TPU v7x, 512 devices: a whole 4x4x16 slice. The times are simulated.
512 devices in a mesh: depth: 16 (over z), lat: 32 (over x, y, core).
Axes of the slice: x: 4, y: 4, z: 16, core: 2. Of those that a mesh axis runs over, the one named last changes fastest.
Arguments:
- volume: float32 [4, 64, 512, 512], P(None, 'depth', 'lat'), may hold values from 0 to 2
- offsets: int32 [8, 64], P(None, 'depth'), may hold values from -4 to 4, as said below
- view_ids: int32 [2], replicated, may hold values from 0 to 7
- weights: float32 [2, 4, 512, 512], P(None, None, 'lat'), may hold values from -6 to 6
Outputs:
- image_out: float32 [2, 4, 512, 512], P(None, None, 'lat')
- grad_out: float32 [4, 64, 512, 512], P(None, 'depth', 'lat')
Inputs may be any that keep to these rules, and one draw needn't show every extreme that they name: `offsets`: in every pose some slice has offset 4 and another has offset -4.
All inputs are finite; a program needn't handle non-finite values.
Results may differ from a plain program's by a relative error of at most 0.00017.
Values sent between devices are 32-bit elements; how exact they have to be, the bound alone decides.
No kernel may reach another device: no remote copies, remote signals or barrier semaphores. Data moves between devices by JAX's collectives and lax.ppermute only.
A program may use at most 64 MiB of HBM per device.

v0:
```python
import jax
import jax.numpy as jnp
from jax import lax
from jax.sharding import PartitionSpec as P

HALO = 4


def padded_2(block, sides, width):
    for axis, dim in sides:
        count = lax.axis_size(axis)
        forward = [(i, i + 1) for i in range(count - 1)]
        backward = [(target, source) for source, target in forward]
        low = lax.ppermute(
            lax.slice_in_dim(block, block.shape[dim] - width, None, axis=dim), axis, forward
        )
        high = lax.ppermute(lax.slice_in_dim(block, 0, width, axis=dim), axis, backward)
        block = jnp.concatenate([low, block, high], axis=dim)
    return block


def prefix(value, axis, join, neutral, backward):
    count, mine = (lax.axis_size(axis), lax.axis_index(axis))
    pieces = jax.tree.map(lambda part: lax.all_gather(part, axis), value)
    if backward:
        pieces = jax.tree.map(lambda part: part[::-1], pieces)
        mine = count - 1 - mine
    subtotal = jax.tree.map(
        lambda part, zero: jnp.full_like(part, 0) + jnp.asarray(zero, part.dtype), value, neutral
    )

    def step(position, subtotal):
        longer = join(subtotal, jax.tree.map(lambda part: part[position], pieces))
        return jax.tree.map(lambda new, old: jnp.where(position < mine, new, old), longer, subtotal)

    return lax.fori_loop(0, count - 1, step, subtotal)


def shear_slices(padded, slice_shift, row_count):

    def one_slice(layer_rows, offset_row):
        return lax.dynamic_slice_in_dim(layer_rows, HALO - offset_row, row_count, 1)

    return jax.vmap(one_slice, in_axes=(1, 0), out_axes=0)(padded, slice_shift)


def join_front(earlier, later):
    return earlier * later


def join_back(behind_part, front_part):
    return (front_part[0] + front_part[1] * behind_part[0], front_part[1] * behind_part[1])


def on_device(volume, offsets, view_ids, weights):
    slab_count = volume.shape[1]
    strip_rows = volume.shape[2]
    depth_total = slab_count * lax.axis_size("depth")
    view_count = view_ids.shape[0]
    select = (view_ids[:, None] == jnp.arange(offsets.shape[0])[None, :]).astype(jnp.int32)
    view_shift = jnp.sum(select[:, :, None] * offsets[None, :, :], axis=1)
    margin = 0
    padded = padded_2(volume, (("lat", 2),), HALO + margin)
    row_count = strip_rows + 2 * margin
    sheared = jnp.stack(
        [shear_slices(padded, view_shift[view_num], row_count) for view_num in range(view_count)],
        axis=1,
    )
    absorb = 1.0 - jnp.exp(-sheared[:, :, 3] / depth_total)
    glow_term = jnp.sum(sheared[:, :, :3] * weights[None, :, :3], axis=2)
    all_ones = jnp.ones(absorb.shape[1:], jnp.float32)
    all_zeros = jnp.zeros(absorb.shape[1:], jnp.float32)

    def front_step(carried, element):
        transmit, radiance = carried
        alpha_k, emission = element
        return (
            (transmit * (1.0 - alpha_k), radiance + (transmit * alpha_k)[:, None] * emission),
            transmit,
        )

    zeros_colour = jnp.zeros((view_count, 3) + absorb.shape[2:], jnp.float32)
    (slab_trans, slab_colour), trans_loc = lax.scan(
        front_step, (all_ones, zeros_colour), (absorb, sheared[:, :, :3])
    )

    def back_step(carried, element):
        comp_part, keep_part = carried
        alpha_k, glow_k = element
        return (
            (alpha_k * glow_k + (1.0 - alpha_k) * comp_part, (1.0 - alpha_k) * keep_part),
            (comp_part, keep_part),
        )

    (slab_comp, slab_keep), (comp_after, keep_after) = lax.scan(
        back_step, (all_zeros, all_ones), (absorb, glow_term), reverse=True
    )
    trans_in = prefix(slab_trans, "depth", join_front, all_ones, False)
    colours, opacity = lax.psum(
        (trans_in[:, None] * slab_colour, trans_in * (1.0 - slab_trans)), "depth"
    )
    comp_in, keep_in = prefix(
        (slab_comp, slab_keep), "depth", join_back, (all_zeros, all_ones), True
    )
    enter = comp_in - keep_in * weights[:, 3]
    image_out = jnp.concatenate([colours, opacity[:, None]], axis=1)
    trans_full = trans_in[None] * trans_loc
    behind = comp_after + keep_after * enter[None]
    grad_emit = depth_total * (trans_full * absorb)[:, :, None] * weights[None, :, :3]
    grad_absorb = (1.0 - absorb) * trans_full * (glow_term - behind)
    grad_img = jnp.concatenate([grad_emit, grad_absorb[:, :, None]], axis=2)
    grad_img = padded_2(grad_img, (("lat", 3),), HALO)

    def unshear(slice_grad, slice_shift):
        summed = jnp.zeros((4, strip_rows, slice_grad.shape[3]), jnp.float32)
        for view_num in range(view_count):
            summed = summed + lax.dynamic_slice_in_dim(
                slice_grad[view_num], HALO + slice_shift[view_num], strip_rows, 1
            )
        return summed

    grad_out = jax.vmap(unshear, in_axes=(0, 1), out_axes=1)(grad_img, view_shift)
    return (image_out, grad_out)


def solution(mesh):
    in_specs = (P(None, "depth", "lat", None), P(None, "depth"), P(), P(None, None, "lat", None))
    out_specs = (P(None, None, "lat", None), P(None, "depth", "lat", None))
    return jax.shard_map(
        on_device, mesh=mesh, in_specs=in_specs, out_specs=out_specs, check_vma=False
    )
```

profile of v0, /device:TPU:6, one launch (start us, length us, event | category | flops | bytes accessed | tf_op | source)
XLA Modules:
  0.0 393.3 jit_solution(15331093073666863692)
XLA Ops:
  7.2 1.4 copy.40
  8.7 1.9 collective-permute-start
  10.6 5.8 %collective-permute-start.1 = (f32[4,4,4,512]{3,0,1,2:T(4,128)S(1)}, f32[4,4,4,512]{3,0,1,2:T(4,128)S(1)}, u32[]{:S(2)}, u32[]{:S(2)}) collective-permute-start(f32[4,4,4,512]{3,0,1,2:T(4,128)S(1)} %get-tuple-element.570), channel_id=1, source_target_pairs={{1,0},{2,1},{3,2},{4,3},{5,4},{6,5},{7,6},{8,7},{9,8},{10,9},{11,1... | collective-permute-start | bytes 393224 | tf_op jit(solution)/shard_map/ppermute | solution.py:17
  16.4 0.1 compare_convert_fusion
  16.5 0.1 copy.47
  16.7 0.1 multiply_reduce_fusion.1
  16.8 0.3 collective-permute-done
  17.1 1.8 collective-permute-done.1
  18.9 0.3 maximum_bitcast_fusion
  19.2 0.9 gather_fusion.1
  20.1 0.9 gather_fusion
  20.9 0.3 pad_maximum_fusion.4
  21.4 0.9 multiply_reduce_fusion
  22.3 0.2 copy.45
  22.6 0.4 while.68
  23.0 0.6 copy-done.3
  23.7 0.5 while.66
  23.7 0.1 fusion.17
  23.9 0.1 fusion.17
  24.2 0.6 copy-done
  24.9 0.6 all-gather.11.cloned.1.call-update
  25.6 73.7 %all-gather.9.cloned.1.call-done = f32[32,16,512]{2,1,0:T(8,128)} async-done(((f32[2,16,512]{2,1,0:T(8,128)}), f32[32,16,512]{2,1,0:T(8,128)}) %all-gather.9.cloned.1.call-update) | async-done | bytes 1048592 | tf_op jit(solution)/shard_map/all_gather | solution.py:24
  99.4 1.3 rev.6
  100.7 68.5 %all-gather.7.cloned.1.call-done = f32[32,16,512]{2,1,0:T(8,128)} async-done(((f32[2,16,512]{2,1,0:T(8,128)}), f32[32,16,512]{2,1,0:T(8,128)}) %all-gather.7.cloned.1.call-update) | async-done | bytes 1048592 | tf_op jit(solution)/shard_map/all_gather | solution.py:24
  169.2 13.3 %while.67 = (s32[]{:T(128)}, f32[2,16,512]{2,1,0:T(8,128)S(1)}, s32[]{:T(128)}, f32[16,2,16,512]{3,2,1,0:T(8,128)}, s32[]{:T(128)}, /*index=5*/s32[]{:T(128)}) while((s32[]{:T(128)}, f32[2,16,512]{2,1,0:T(8,128)S(1)}, s32[]{:T(128)}, f32[16,2,16,512]{3,2,1,0:T(8,128)}, s32[]{:T(128)}, /*index=5*/s32[]{:T(128)}) %tuple.164), condition=%wide.region_4.5_spmd.clone, body=%wide.region_3.4_spmd.clone.sunk | while | flops 49156 | bytes 196709 | solution.py:36
  169.2 0.9 multiply_select_fusion.4
  170.1 0.9 multiply_select_fusion.4
  170.9 0.9 multiply_select_fusion.4
  171.8 0.9 multiply_select_fusion.4
  172.7 0.9 multiply_select_fusion.4
  173.6 0.9 multiply_select_fusion.4
  174.5 0.9 multiply_select_fusion.4
  175.4 0.9 multiply_select_fusion.4
  176.3 0.9 multiply_select_fusion.4
  177.1 0.9 multiply_select_fusion.4
  178.0 0.9 multiply_select_fusion.4
  178.9 0.9 multiply_select_fusion.4
  179.8 0.9 multiply_select_fusion.4
  180.7 0.9 multiply_select_fusion.4
  181.6 0.9 multiply_select_fusion.4
  182.5 56.5 %all-gather.11.cloned.1.call-done = f32[32,16,512]{2,1,0:T(8,128)} async-done(((f32[2,16,512]{2,1,0:T(8,128)}), f32[32,16,512]{2,1,0:T(8,128)}) %all-gather.11.cloned.1.call-update) | async-done | bytes 1048592 | tf_op jit(solution)/shard_map/all_gather | solution.py:24
  239.0 1.3 rev.7
  240.3 1.1 while.69
  241.4 0.9 fusion.10
  242.2 1.2 multiply_multiply_fusion
  243.4 0.2 broadcast_in_dim.52
  243.6 0.2 broadcast_multiply_fusion
  243.8 0.2 pad_maximum_fusion.3
  244.1 1.9 collective-permute-start.2
  246.0 5.8 %collective-permute-start.3 = (f32[4,2,4,4,512]{4,2,3,0,1:T(4,128)S(1)}, f32[4,2,4,4,512]{4,2,3,0,1:T(4,128)S(1)}, u32[]{:S(2)}, u32[]{:S(2)}) collective-permute-start(f32[4,2,4,4,512]{4,2,3,0,1:T(4,128)S(1)} %get-tuple-element.564), channel_id=1, source_target_pairs={{1,0},{2,1},{3,2},{4,3},{5,4},{6,5},{7,6},{8,7},{9,8},{10,9},{11,1... | collective-permute-start | bytes 786440 | tf_op jit(solution)/shard_map/ppermute | solution.py:17
  251.8 0.6 multiply_bitcast_fusion
  252.4 0.7 broadcast_multiply_fusion.1
  253.1 0.8 collective-permute-done.2
  253.9 1.8 collective-permute-done.3
  255.6 0.6 pad_maximum_fusion
  256.2 0.3 slice_bitcast_fusion
  256.6 0.1 copy.54
  256.7 0.1 copy.53
  256.7 0.9 gather_fusion.3
  257.6 0.9 gather_fusion.2
  258.5 0.1 add_bitcast_fusion
  258.6 1.0 copy.55
  259.6 125.5 %all-reduce.3.cloned.1.call-done = (f32[2,1,16,512]{3,2,1,0:T(8,128)}, f32[2,3,16,512]{3,2,1,0:T(8,128)}) async-done(((f32[2,1,16,512]{3,2,1,0:T(8,128)}, f32[2,3,16,512]{3,2,1,0:T(8,128)}), (f32[2,1,16,512]{3,2,1,0:T(8,128)}, f32[2,3,16,512]{3,2,1,0:T(8,128)})) %all-reduce.3.cloned.1.call-update) | async-done | bytes 262160 | tf_op jit(solution)/shard_map/psum | solution.py:99
  385.0 1.7 pad_maximum_fusion.5
  (70 shorter events, 1.6 us)
Async XLA Ops:
  7.2 9.3 %copy-start.7 = (s32[2]{0:T(128)S(1)}, s32[2]{0:T(128)}, u32[]{:S(2)}) copy-start(s32[2]{0:T(128)} %param.14) | copy-start | bytes 28
  7.2 9.3 %slice-start = ((f32[2,4,16,512]{3,2,1,0:T(8,128)}), f32[2,3,16,512]{3,2,1,0:T(8,128)S(1)}, s32[]{:S(2)}) async-start(f32[2,4,16,512]{3,2,1,0:T(8,128)} %param.15), calls=%async_computation.4 | async-start | bytes 393216 | tf_op jit(solution)/shard_map/slice | solution.py:109
  7.2 9.5 %copy-start.6 = (s32[8,4]{0,1:T(4,128)S(1)}, s32[8,4]{0,1:T(4,128)}, u32[]{:S(2)}) copy-start(s32[8,4]{0,1:T(4,128)} %param.13) | copy-start | bytes 388
  7.2 92.2 %all-gather.9.cloned.1.call-start = ((), (), s32[]{:S(2)}) async-start(), calls=%async_computation.1 | async-start | bytes 1114112 | tf_op jit(solution)/shard_map/all_gather | solution.py:24
  8.7 8.4 %collective-permute-start = (f32[4,4,4,512]{3,0,1,2:T(4,128)S(1)}, f32[4,4,4,512]{3,0,1,2:T(4,128)S(1)}, u32[]{:S(2)}, u32[]{:S(2)}) collective-permute-start(f32[4,4,4,512]{3,0,1,2:T(4,128)S(1)} %get-tuple-element.569), channel_id=1, source_target_pairs={{0,1},{1,2},{2,3},{3,4},{4,5},{5,6},{6,7},{7,8},{8,9},{9,10},{10,1... | collective-permute-start | bytes 393224 | tf_op jit(solution)/shard_map/ppermute | solution.py:14
  10.6 8.3 %collective-permute-start.1 = (f32[4,4,4,512]{3,0,1,2:T(4,128)S(1)}, f32[4,4,4,512]{3,0,1,2:T(4,128)S(1)}, u32[]{:S(2)}, u32[]{:S(2)}) collective-permute-start(f32[4,4,4,512]{3,0,1,2:T(4,128)S(1)} %get-tuple-element.570), channel_id=1, source_target_pairs={{1,0},{2,1},{3,2},{4,3},{5,4},{6,5},{7,6},{8,7},{9,8},{10,9},{11,1... | collective-permute-start | bytes 393224 | tf_op jit(solution)/shard_map/ppermute | solution.py:17
  22.9 0.6 copy-start.3
  22.9 0.7 copy-start.2
  23.0 216.0 %copy-start.4 = (f32[4,2,16,512]{3,2,0,1:T(8,128)}, f32[4,2,16,512]{3,2,0,1:T(8,128)S(1)}, u32[]{:S(2)}) copy-start(f32[4,2,16,512]{3,2,0,1:T(8,128)S(1)} %get-tuple-element.374) | copy-start | bytes 786436
  23.6 145.6 %all-gather.7.cloned.1.call-start = ((), (), s32[]{:S(2)}) async-start(), calls=%async_computation | async-start | bytes 1114112 | tf_op jit(solution)/shard_map/all_gather | solution.py:24
  24.2 0.6 copy-start
  24.2 214.8 %copy-start.5 = (f32[4,2,16,512]{3,2,0,1:T(8,128)}, f32[4,2,16,512]{3,2,0,1:T(8,128)S(1)}, u32[]{:S(2)}) copy-start(f32[4,2,16,512]{3,2,0,1:T(8,128)S(1)} %get-tuple-element.372) | copy-start | bytes 786436
  24.9 214.1 %all-gather.11.cloned.1.call-start = ((), (), s32[]{:S(2)}) async-start(), calls=%async_computation.2 | async-start | bytes 1114112 | tf_op jit(solution)/shard_map/all_gather | solution.py:24
  25.6 359.5 %all-reduce.3.cloned.1.call-start = ((), (), s32[]{:S(2)}) async-start(), calls=%async_computation.3 | async-start | bytes 524288 | tf_op jit(solution)/shard_map/psum | solution.py:99
  243.6 8.2 %copy-start.1 = (f32[2,16,512]{2,1,0:T(8,128)S(1)}, f32[2,16,512]{2,1,0:T(8,128)}, u32[]{:S(2)}) copy-start(f32[2,16,512]{2,1,0:T(8,128)} %copy-done) | copy-start | bytes 196612
  244.1 9.8 %collective-permute-start.2 = (f32[4,2,4,4,512]{4,2,3,0,1:T(4,128)S(1)}, f32[4,2,4,4,512]{4,2,3,0,1:T(4,128)S(1)}, u32[]{:S(2)}, u32[]{:S(2)}) collective-permute-start(f32[4,2,4,4,512]{4,2,3,0,1:T(4,128)S(1)} %get-tuple-element.563), channel_id=1, source_target_pairs={{0,1},{1,2},{2,3},{3,4},{4,5},{5,6},{6,7},{7,8},{8,9},{9,10},{10,1... | collective-permute-start | bytes 786440 | tf_op jit(solution)/shard_map/ppermute | solution.py:14
  246.0 9.6 %collective-permute-start.3 = (f32[4,2,4,4,512]{4,2,3,0,1:T(4,128)S(1)}, f32[4,2,4,4,512]{4,2,3,0,1:T(4,128)S(1)}, u32[]{:S(2)}, u32[]{:S(2)}) collective-permute-start(f32[4,2,4,4,512]{4,2,3,0,1:T(4,128)S(1)} %get-tuple-element.564), channel_id=1, source_target_pairs={{1,0},{2,1},{3,2},{4,3},{5,4},{6,5},{7,6},{8,7},{9,8},{10,9},{11,1... | collective-permute-start | bytes 786440 | tf_op jit(solution)/shard_map/ppermute | solution.py:17
Sparse Core Ops, SparseCore 0:
  23.7 75.6 all-gather.8
  101.5 67.6 all-gather.6
  171.3 67.6 all-gather.10
  253.3 131.7 all-reduce.2
where the time goes:
time: 394 us; the launch traced here: 393 us
  waiting for transfers between devices  329 us (84%)
  other arithmetic  22.3 us (6%)
  starting transfers between devices  15.5 us (4%)
  between operations  14.2 us (4%)
  local copies, waits for them, and re-layouts  10.8 us (3%)
    all_gather x3, waiting for transfers between devices, prefix(): pieces = jax.tree.map(lambda part: lax.all_gather(part, axis), value)  199 us
    psum x1, waiting for transfers between devices, on_device(): lax.psum((trans_in[:, None] * slab_colour, trans_in * (1.0 - slab_trans))...  125 us
    select_n x30, other arithmetic, step(): jnp.where(position < mine, new, old)  13.6 us
    ppermute x2, starting transfers between devices, padded_2(): lax.ppermute(lax.slice_in_dim(block, 0, width, axis=dim), axis, backward)  11.5 us
  transfers between devices with their start and end apart: 8, of which 8 were waited for; matrix products, arithmetic and copies ran while one was open for 5% of the time, Pallas kernels for 0%

commit v1 on v0

v1 whole, which is shorter than its diff:
```python
import jax
import jax.numpy as jnp
from jax import lax
from jax.experimental import pallas as pl
from jax.experimental.pallas import tpu as pltpu
from jax.sharding import PartitionSpec as P

HALO = 4
LANES = 128
VMEM = pl.BlockSpec(memory_space=pltpu.VMEM)
SMEM = pl.BlockSpec(memory_space=pltpu.SMEM)


def slab_kernel(
    depth_total, offs, vids, vol, low, high, w, agg, absorb_part, emit_part, ext
):
    channels, slabs, rows, cols = vol.shape
    views = w.shape[0]
    tiles = cols // LANES
    bands = rows // 8
    for c in range(channels):
        for k in range(slabs):
            for t in range(tiles):
                lanes = pl.ds(t * LANES, LANES)
                ext[c, k, t, 4:8, :] = low[c, k, :, lanes]
                ext[c, k, t, 8 : 8 + rows, :] = vol[c, k, :, lanes]
                ext[c, k, t, 8 + rows : 12 + rows, :] = high[c, k, :, lanes]
    for v in range(views):
        starts = [8 - offs[k, vids[v]] for k in range(slabs)]
        for t in range(tiles):
            lanes = pl.ds(t * LANES, LANES)
            weight = [w[v, c, :, lanes] for c in range(3)]
            transmit = jnp.ones((rows, LANES), jnp.float32)
            colour = [jnp.zeros((rows, LANES), jnp.float32) for _ in range(3)]
            alphas, keeps, glows, fronts = [], [], [], []
            for k in range(slabs):
                part = [ext[c, k, t, pl.ds(starts[k], rows), :] for c in range(channels)]
                keep = jnp.exp(part[3] * (-1.0 / depth_total))
                alpha = 1.0 - keep
                seen = transmit * alpha
                colour = [colour[c] + seen * part[c] for c in range(3)]
                emit_part[v, k, t] = seen * float(depth_total)
                glows.append(weight[0] * part[0] + weight[1] * part[1] + weight[2] * part[2])
                alphas.append(alpha)
                keeps.append(keep)
                transmit = transmit * keep
                fronts.append(transmit)
            behind = jnp.zeros((rows, LANES), jnp.float32)
            for k in range(slabs - 1, -1, -1):
                absorb_part[v, k, t] = fronts[k] * (glows[k] - behind)
                behind = alphas[k] * glows[k] + keeps[k] * behind
            for b in range(bands):
                owner = (v * bands + b) * tiles + t
                agg[owner, 0] = transmit[8 * b : 8 * b + 8]
                for c in range(3):
                    agg[owner, 1 + c] = colour[c][8 * b : 8 * b + 8]


def scan_kernel(place, agg, w, out):
    count = agg.shape[0]
    transmit = jnp.ones((8, LANES), jnp.float32)
    colour = [jnp.zeros((8, LANES), jnp.float32) for _ in range(3)]
    entering = []
    for s in range(count):
        entering.append(transmit)
        colour = [colour[c] + transmit * agg[s, 1 + c] for c in range(3)]
        transmit = transmit * agg[s, 0]
    opacity = 1.0 - transmit
    behind = -w[0, 3]
    for s in range(count - 1, -1, -1):
        passed = agg[s, 0] * behind
        out[s, 0] = entering[s]
        out[s, 1] = entering[s] * passed
        for c in range(3):
            out[s, 2 + c] = colour[c]
        out[s, 5] = opacity
        glow = w[0, 0] * agg[s, 1] + w[0, 1] * agg[s, 2] + w[0, 2] * agg[s, 3]
        behind = glow + passed


def grad_kernel(
    offs, vids, got, absorb_part, emit_part, w, main, low, high, image, shifted
):
    views, channels, rows, cols = w.shape
    slabs = main.shape[1]
    tiles = cols // LANES
    bands = rows // 8
    edge = jnp.zeros((8, LANES), jnp.float32)
    for v in range(views):
        for t in range(tiles):
            lanes = pl.ds(t * LANES, LANES)
            owners = [(v * bands + b) * tiles + t for b in range(bands)]
            front = jnp.concatenate([got[n, 0] for n in owners], axis=0)
            passed = jnp.concatenate([got[n, 1] for n in owners], axis=0)
            for b, n in enumerate(owners):
                for c in range(channels):
                    image[v, c, 8 * b : 8 * b + 8, lanes] = got[n, 2 + c]
            weight = [front * w[v, c, :, lanes] for c in range(3)]
            for k in range(slabs):
                emit = emit_part[v, k, t]
                parts = [emit * weight[c] for c in range(3)]
                parts.append(front * absorb_part[v, k, t] - passed)
                for c in range(channels):
                    shifted[v, k, c, t, 0:8, :] = edge
                    shifted[v, k, c, t, 8 : 8 + rows, :] = parts[c]
                    shifted[v, k, c, t, 8 + rows : 16 + rows, :] = edge
    for k in range(slabs):
        moves = [offs[k, vids[v]] for v in range(views)]
        for c in range(channels):
            for t in range(tiles):
                lanes = pl.ds(t * LANES, LANES)

                def total(start, size):
                    return sum(
                        shifted[v, k, c, t, pl.ds(start + moves[v], size), :]
                        for v in range(views)
                    )

                low[c, k, :, lanes] = total(4, 4)
                main[c, k, :, lanes] = total(8, rows)
                high[c, k, :, lanes] = total(8 + rows, 4)


def join_kernel(main, low, high, out):
    rows = main.shape[2]
    out[:, :, 0:4, :] = main[:, :, 0:4, :] + low[...]
    out[:, :, 4 : rows - 4, :] = main[:, :, 4 : rows - 4, :]
    out[:, :, rows - 4 :, :] = main[:, :, rows - 4 :, :] + high[...]


def on_device(volume, offsets, view_ids, weights):
    channels, slabs, rows, cols = volume.shape
    views = weights.shape[0]
    count = lax.axis_size("depth")
    strips = lax.axis_size("lat")
    tiles, bands = cols // LANES, rows // 8
    depth_total = slabs * count
    up = [(i, i + 1) for i in range(strips - 1)]
    down = [(i + 1, i) for i in range(strips - 1)]
    f32 = lambda *shape: jax.ShapeDtypeStruct(shape, jnp.float32)
    table = offsets.T

    low = lax.ppermute(volume[:, :, rows - HALO :], "lat", up)
    high = lax.ppermute(volume[:, :, :HALO], "lat", down)
    agg, absorb_part, emit_part = pl.pallas_call(
        lambda *refs: slab_kernel(depth_total, *refs),
        out_shape=(
            f32(count, 4, 8, LANES),
            f32(views, slabs, tiles, rows, LANES),
            f32(views, slabs, tiles, rows, LANES),
        ),
        in_specs=[SMEM, SMEM, VMEM, VMEM, VMEM, VMEM],
        out_specs=(VMEM, VMEM, VMEM),
        scratch_shapes=[pltpu.VMEM((channels, slabs, tiles, rows + 16, LANES), jnp.float32)],
        name="slab",
    )(table, view_ids, volume, low, high, weights)

    agg = lax.all_to_all(agg, "depth", 0, 0, tiled=True)
    place = lax.axis_index("depth").reshape(1).astype(jnp.int32)
    sent = pl.pallas_call(
        scan_kernel,
        out_shape=f32(count, 6, 8, LANES),
        grid_spec=pltpu.PrefetchScalarGridSpec(
            num_scalar_prefetch=1,
            grid=(1,),
            in_specs=[
                pl.BlockSpec((count, 4, 8, LANES), lambda i, z: (0, 0, 0, 0)),
                pl.BlockSpec(
                    (1, 4, 8, LANES),
                    lambda i, z: (z[0] // (bands * tiles), 0, (z[0] // tiles) % bands, z[0] % tiles),
                ),
            ],
            out_specs=pl.BlockSpec((count, 6, 8, LANES), lambda i, z: (0, 0, 0, 0)),
        ),
        name="scan",
    )(place, agg, weights)
    got = lax.all_to_all(sent, "depth", 0, 0, tiled=True)

    main, to_low, to_high, image_out = pl.pallas_call(
        grad_kernel,
        out_shape=(
            f32(channels, slabs, rows, cols),
            f32(channels, slabs, HALO, cols),
            f32(channels, slabs, HALO, cols),
            f32(views, channels, rows, cols),
        ),
        in_specs=[SMEM, SMEM, VMEM, VMEM, VMEM, VMEM],
        out_specs=(VMEM, VMEM, VMEM, VMEM),
        scratch_shapes=[
            pltpu.VMEM((views, slabs, channels, tiles, rows + 16, LANES), jnp.float32)
        ],
        name="grad",
    )(table, view_ids, got, absorb_part, emit_part, weights)
    from_low = lax.ppermute(to_high, "lat", up)
    from_high = lax.ppermute(to_low, "lat", down)
    grad_out = pl.pallas_call(
        join_kernel,
        out_shape=f32(channels, slabs, rows, cols),
        in_specs=[VMEM, VMEM, VMEM],
        out_specs=VMEM,
        name="join",
    )(main, from_low, from_high)
    return (image_out, grad_out)


def solution(mesh):
    in_specs = (P(None, "depth", "lat", None), P(None, "depth"), P(), P(None, None, "lat", None))
    out_specs = (P(None, None, "lat", None), P(None, "depth", "lat", None))
    return jax.shard_map(
        on_device, mesh=mesh, in_specs=in_specs, out_specs=out_specs, check_vma=False
    )
```

time: 394 us -> 96 us (0.24)
  the two profiles are of different devices: /device:TPU:6 before, /device:TPU:19 now
where the time goes in v1:
time: 96 us; the launch traced here: 95.6 us
  starting transfers between devices  36.2 us (38%)
  blocking collectives  27.8 us (29%)
  waiting for transfers between devices  19.2 us (20%)
  Pallas kernels  8.57 us (9%)
  local copies, waits for them, and re-layouts  3.09 us (3%)
    all_to_all x1, blocking collectives, on_device(): got = lax.all_to_all(sent, 'depth', 0, 0, tiled=True)  27.8 us
    all_to_all x1, starting transfers between devices, on_device(): agg = lax.all_to_all(agg, 'depth', 0, 0, tiled=True)  14.9 us
    ppermute x1, starting transfers between devices, on_device(): from_low = lax.ppermute(to_high, 'lat', up)  13.8 us
    all_to_all x1, waiting for transfers between devices, on_device(): agg = lax.all_to_all(agg, 'depth', 0, 0, tiled=True)  12.7 us
    ppermute x1, waiting for transfers between devices, on_device(): from_high = lax.ppermute(to_low, 'lat', down)  4.25 us
    ppermute x1, starting transfers between devices, on_device(): low = lax.ppermute(volume[:, :, rows - HALO:], 'lat', up)  2.98 us
    ppermute x1, starting transfers between devices, on_device(): high = lax.ppermute(volume[:, :, :HALO], 'lat', down)  2.58 us
    pallas_call x1, Pallas kernels, on_device(): pl.pallas_call(grad_kernel, out_shape=(f32(channels, slabs, rows, cols),...  2.48 us
  transfers between devices with their start and end apart: 5, of which 5 were waited for; matrix products, arithmetic and copies ran while one was open for 0% of the time, Pallas kernels for 0%

profile of v1, /device:TPU:19, one launch (start us, length us, event | category | flops | bytes accessed | tf_op | source)
XLA Modules:
  0.0 95.6 jit_solution(10173404069152923987)
XLA Ops:
  0.6 1.1 %fusion = (f32[4,4,4,512]{3,2,1,0:T(4,128)S(1)}, f32[4,4,4,512]{3,2,1,0:T(4,128)S(1)}) fusion(f32[4,4,16,512]{3,2,1,0:T(8,128)} %refs_2_.1), kind=kLoop, calls=%fused_computation | loop fusion | bytes 524288 | tf_op jit(solution)/shard_map/slice | solution.py:144
  1.7 2.6 %collective-permute-start.1 = (f32[4,4,4,512]{3,2,1,0:T(4,128)S(1)}, f32[4,4,4,512]{3,2,1,0:T(4,128)S(1)}, u32[]{:S(2)}, u32[]{:S(2)}) collective-permute-start(f32[4,4,4,512]{3,2,1,0:T(4,128)S(1)} %get-tuple-element.16), channel_id=1, source_target_pairs={{1,0},{2,1},{3,2},{4,3},{5,4},{6,5},{7,6},{8,7},{9,8},{10,9},{11,1... | collective-permute-start | bytes 393224 | tf_op jit(solution)/shard_map/ppermute | solution.py:144
  4.3 3.0 %collective-permute-start = (f32[4,4,4,512]{3,2,1,0:T(4,128)S(1)}, f32[4,4,4,512]{3,2,1,0:T(4,128)S(1)}, u32[]{:S(2)}, u32[]{:S(2)}) collective-permute-start(f32[4,4,4,512]{3,2,1,0:T(4,128)S(1)} %get-tuple-element.17), channel_id=1, source_target_pairs={{0,1},{1,2},{2,3},{3,4},{4,5},{5,6},{6,7},{7,8},{8,9},{9,10},{10,1... | collective-permute-start | bytes 393224 | tf_op jit(solution)/shard_map/ppermute | solution.py:143
  7.3 0.7 collective-permute-done.1.refs_4_
  8.0 0.0 copy-start.3
  8.0 1.2 %collective-permute-done.refs_3_ = f32[4,4,4,512]{3,2,1,0:T(4,128)S(1)} collective-permute-done((f32[4,4,4,512]{3,2,1,0:T(4,128)S(1)}, f32[4,4,4,512]{3,2,1,0:T(4,128)S(1)}, u32[]{:S(2)}, u32[]{:S(2)}) %collective-permute-start) | collective-permute-done | bytes 131104 | tf_op jit(solution)/shard_map/ppermute | solution.py:143
  9.2 0.0 copy-start.4
  9.2 0.0 copy-done.3
  9.2 0.7 copy-done.4
  9.9 2.3 %slab.1 = (f32[16,4,8,128]{3,2,1,0:T(8,128)}, f32[2,4,4,16,128]{4,3,2,1,0:T(8,128)}, f32[2,4,4,16,128]{4,3,2,1,0:T(8,128)}) custom-call(s32[4,8]{1,0:T(4,128)} %bitcast.2, s32[2]{0:T(128)} %vids.1, f32[4,4,16,512]{3,2,1,0:T(8,128)} %refs_2_.1, f32[4,4,4,512]{3,2,1,0:T(4,128)} %copy-done.4, f32[4,4,4,512]{3,2,1,0:T(4,128)} %copy-done.3, f32[2,4,16,512]{3,2,1,0:T(8,128)} %w.3), custom_call_target="tpu_custom_call" | custom-call | tf_op jit(solution)/shard_map/slab/pallas_call | solution.py:145
  12.2 14.9 %all-to-all-start = ((f32[16,4,8,128]{3,2,1,0:T(8,128)}), f32[16,4,8,128]{3,2,1,0:T(8,128)S(1)}, u32[]{:S(2)}, u32[]{:S(2)}) async-start(f32[16,4,8,128]{3,2,1,0:T(8,128)} %get-tuple-element.9), calls=%async_computation | async-start | bytes 524288 | tf_op jit(solution)/shard_map/all_to_all | solution.py:158
  27.1 12.7 %all-to-all-done.agg = f32[16,4,8,128]{3,2,1,0:T(8,128)S(1)} async-done(((f32[16,4,8,128]{3,2,1,0:T(8,128)}), f32[16,4,8,128]{3,2,1,0:T(8,128)S(1)}, u32[]{:S(2)}, u32[]{:S(2)}) %all-to-all-start) | async-done | bytes 262176 | tf_op jit(solution)/shard_map/all_to_all | solution.py:158
  39.8 0.0 copy-start
  39.9 0.7 copy-done
  40.6 1.8 %scan.1 = f32[16,6,8,128]{3,2,1,0:T(8,128)} custom-call(s32[1]{0:T(128)} %bitcast.1.place, f32[16,4,8,128]{3,2,1,0:T(8,128)} %copy-done, f32[2,4,16,512]{3,2,1,0:T(8,128)} %w.3), custom_call_target="tpu_custom_call" | custom-call | tf_op jit(solution)/shard_map/scan/pallas_call | solution.py:160
  42.3 27.8 %all_to_all.10.got = f32[16,6,8,128]{3,2,1,0:T(8,128)} all-to-all(f32[16,6,8,128]{3,2,1,0:T(8,128)} %scan.1), channel_id=1, replica_groups=mesh['depth'=16,'lat'=32] {'depth'}, dimensions={0} | all-to-all | bytes 786432 | tf_op jit(solution)/shard_map/all_to_all | solution.py:177
  70.1 2.5 %grad.1 = (f32[4,4,16,512]{3,2,1,0:T(8,128)}, f32[4,4,4,512]{3,2,1,0:T(4,128)}, f32[4,4,4,512]{3,2,1,0:T(4,128)}, f32[2,4,16,512]{3,2,1,0:T(8,128)}) custom-call(s32[4,8]{1,0:T(4,128)} %bitcast.3, s32[2]{0:T(128)} %vids.1, f32[16,6,8,128]{3,2,1,0:T(8,128)} %all_to_all.10.got, f32[2,4,4,16,128]{4,3,2,1,0:T(8,128)} %get-tuple-element.10.absorb_part, ...), custom_call_target="tpu_custom_call" | custom-call | tf_op jit(solution)/shard_map/grad/pallas_call | solution.py:179
  72.6 13.8 %collective-permute-start.2 = (f32[4,4,4,512]{3,2,1,0:T(4,128)}, f32[4,4,4,512]{3,2,1,0:T(4,128)S(1)}, u32[]{:S(2)}, u32[]{:S(2)}) collective-permute-start(f32[4,4,4,512]{3,2,1,0:T(4,128)} %get-tuple-element.14), channel_id=1, source_target_pairs={{0,1},{1,2},{2,3},{3,4},{4,5},{5,6},{6,7},{7,8},{8,9},{9,10},{10,1... | collective-permute-start | bytes 393224 | tf_op jit(solution)/shard_map/ppermute | solution.py:194
  86.4 1.9 %collective-permute-start.3 = (f32[4,4,4,512]{3,2,1,0:T(4,128)}, f32[4,4,4,512]{3,2,1,0:T(4,128)S(1)}, u32[]{:S(2)}, u32[]{:S(2)}) collective-permute-start(f32[4,4,4,512]{3,2,1,0:T(4,128)} %get-tuple-element.15), channel_id=1, source_target_pairs={{1,0},{2,1},{3,2},{4,3},{5,4},{6,5},{7,6},{8,7},{9,8},{10,9},{11,1... | collective-permute-start | bytes 393224 | tf_op jit(solution)/shard_map/ppermute | solution.py:195
  88.3 0.3 collective-permute-done.2.low
  88.6 0.0 copy-start.1
  88.6 4.3 %collective-permute-done.3.high = f32[4,4,4,512]{3,2,1,0:T(4,128)S(1)} collective-permute-done((f32[4,4,4,512]{3,2,1,0:T(4,128)}, f32[4,4,4,512]{3,2,1,0:T(4,128)S(1)}, u32[]{:S(2)}, u32[]{:S(2)}) %collective-permute-start.3) | collective-permute-done | bytes 131104 | tf_op jit(solution)/shard_map/ppermute | solution.py:195
  92.9 0.0 copy-start.2
  92.9 0.0 copy-done.1
  92.9 0.6 copy-done.2
  93.5 2.0 %join.1 = f32[4,4,16,512]{3,2,1,0:T(8,128)} custom-call(f32[4,4,16,512]{3,2,1,0:T(8,128)} %get-tuple-element.13.main, f32[4,4,4,512]{3,2,1,0:T(4,128)} %copy-done.1, f32[4,4,4,512]{3,2,1,0:T(4,128)} %copy-done.2), custom_call_target="tpu_custom_call" | custom-call | tf_op jit(solution)/shard_map/join/pallas_call | solution.py:196
Async XLA Ops:
  1.7 6.3 %collective-permute-start.1 = (f32[4,4,4,512]{3,2,1,0:T(4,128)S(1)}, f32[4,4,4,512]{3,2,1,0:T(4,128)S(1)}, u32[]{:S(2)}, u32[]{:S(2)}) collective-permute-start(f32[4,4,4,512]{3,2,1,0:T(4,128)S(1)} %get-tuple-element.16), channel_id=1, source_target_pairs={{1,0},{2,1},{3,2},{4,3},{5,4},{6,5},{7,6},{8,7},{9,8},{10,9},{11,1... | collective-permute-start | bytes 393224 | tf_op jit(solution)/shard_map/ppermute | solution.py:144
  4.3 4.9 %collective-permute-start = (f32[4,4,4,512]{3,2,1,0:T(4,128)S(1)}, f32[4,4,4,512]{3,2,1,0:T(4,128)S(1)}, u32[]{:S(2)}, u32[]{:S(2)}) collective-permute-start(f32[4,4,4,512]{3,2,1,0:T(4,128)S(1)} %get-tuple-element.17), channel_id=1, source_target_pairs={{0,1},{1,2},{2,3},{3,4},{4,5},{5,6},{6,7},{7,8},{8,9},{9,10},{10,1... | collective-permute-start | bytes 393224 | tf_op jit(solution)/shard_map/ppermute | solution.py:143
  8.0 1.2 %copy-start.3 = (f32[4,4,4,512]{3,2,1,0:T(4,128)}, f32[4,4,4,512]{3,2,1,0:T(4,128)S(1)}, u32[]{:S(2)}) copy-start(f32[4,4,4,512]{3,2,1,0:T(4,128)S(1)} %collective-permute-done.1.refs_4_) | copy-start | bytes 393220
  9.2 0.7 copy-start.4
  12.2 27.6 %all-to-all-start = ((f32[16,4,8,128]{3,2,1,0:T(8,128)}), f32[16,4,8,128]{3,2,1,0:T(8,128)S(1)}, u32[]{:S(2)}, u32[]{:S(2)}) async-start(f32[16,4,8,128]{3,2,1,0:T(8,128)} %get-tuple-element.9), calls=%async_computation | async-start | bytes 524288 | tf_op jit(solution)/shard_map/all_to_all | solution.py:158
  39.8 0.7 copy-start
  72.6 16.1 %collective-permute-start.2 = (f32[4,4,4,512]{3,2,1,0:T(4,128)}, f32[4,4,4,512]{3,2,1,0:T(4,128)S(1)}, u32[]{:S(2)}, u32[]{:S(2)}) collective-permute-start(f32[4,4,4,512]{3,2,1,0:T(4,128)} %get-tuple-element.14), channel_id=1, source_target_pairs={{0,1},{1,2},{2,3},{3,4},{4,5},{5,6},{6,7},{7,8},{8,9},{9,10},{10,1... | collective-permute-start | bytes 393224 | tf_op jit(solution)/shard_map/ppermute | solution.py:194
  86.4 6.5 %collective-permute-start.3 = (f32[4,4,4,512]{3,2,1,0:T(4,128)}, f32[4,4,4,512]{3,2,1,0:T(4,128)S(1)}, u32[]{:S(2)}, u32[]{:S(2)}) collective-permute-start(f32[4,4,4,512]{3,2,1,0:T(4,128)} %get-tuple-element.15), channel_id=1, source_target_pairs={{1,0},{2,1},{3,2},{4,3},{5,4},{6,5},{7,6},{8,7},{9,8},{10,9},{11,1... | collective-permute-start | bytes 393224 | tf_op jit(solution)/shard_map/ppermute | solution.py:195
  88.6 4.3 %copy-start.1 = (f32[4,4,4,512]{3,2,1,0:T(4,128)}, f32[4,4,4,512]{3,2,1,0:T(4,128)S(1)}, u32[]{:S(2)}) copy-start(f32[4,4,4,512]{3,2,1,0:T(4,128)S(1)} %collective-permute-done.2.low) | copy-start | bytes 393220
  92.9 0.7 copy-start.2

commit v2 on v1

v2 whole, which is shorter than its diff:
```python
import jax
import jax.numpy as jnp
from jax import lax
from jax.experimental import pallas as pl
from jax.experimental.pallas import tpu as pltpu
from jax.sharding import PartitionSpec as P

HALO = 4
LANES = 128
VMEM = pl.BlockSpec(memory_space=pltpu.VMEM)
SMEM = pl.BlockSpec(memory_space=pltpu.SMEM)


def slab_kernel(depth_total, offs, vids, vol, low, high, agg, ext):
    channels, slabs, rows, cols = vol.shape
    views = vids.shape[0]
    tiles = cols // LANES
    bands = rows // 8
    for c in range(channels):
        for k in range(slabs):
            for t in range(tiles):
                lanes = pl.ds(t * LANES, LANES)
                ext[c, k, t, 4:8, :] = low[c, k, :, lanes]
                ext[c, k, t, 8 : 8 + rows, :] = vol[c, k, :, lanes]
                ext[c, k, t, 8 + rows : 12 + rows, :] = high[c, k, :, lanes]
    for v in range(views):
        starts = [8 - offs[k, vids[v]] for k in range(slabs)]
        for t in range(tiles):
            transmit = jnp.ones((rows, LANES), jnp.float32)
            colour = [jnp.zeros((rows, LANES), jnp.float32) for _ in range(3)]
            for k in range(slabs):
                part = [ext[c, k, t, pl.ds(starts[k], rows), :] for c in range(channels)]
                keep = jnp.exp(part[3] * (-1.0 / depth_total))
                seen = transmit * (1.0 - keep)
                colour = [colour[c] + seen * part[c] for c in range(3)]
                transmit = transmit * keep
            for b in range(bands):
                owner = (v * bands + b) * tiles + t
                agg[owner, 0] = transmit[8 * b : 8 * b + 8]
                for c in range(3):
                    agg[owner, 1 + c] = colour[c][8 * b : 8 * b + 8]


def local_kernel(depth_total, offs, vids, ext, w, absorb_part, emit_part):
    channels, slabs, tiles = ext.shape[:3]
    views, _, rows, _ = w.shape
    for v in range(views):
        starts = [8 - offs[k, vids[v]] for k in range(slabs)]
        for t in range(tiles):
            lanes = pl.ds(t * LANES, LANES)
            weight = [w[v, c, :, lanes] for c in range(3)]
            transmit = jnp.ones((rows, LANES), jnp.float32)
            alphas, keeps, glows, fronts = [], [], [], []
            for k in range(slabs):
                part = [ext[c, k, t, pl.ds(starts[k], rows), :] for c in range(channels)]
                keep = jnp.exp(part[3] * (-1.0 / depth_total))
                alpha = 1.0 - keep
                emit_part[v, k, t] = transmit * alpha * float(depth_total)
                glows.append(weight[0] * part[0] + weight[1] * part[1] + weight[2] * part[2])
                alphas.append(alpha)
                keeps.append(keep)
                transmit = transmit * keep
                fronts.append(transmit)
            behind = jnp.zeros((rows, LANES), jnp.float32)
            for k in range(slabs - 1, -1, -1):
                absorb_part[v, k, t] = fronts[k] * (glows[k] - behind)
                behind = alphas[k] * glows[k] + keeps[k] * behind


def scan_kernel(place, agg, w, out):
    count = agg.shape[0]
    transmit = jnp.ones((8, LANES), jnp.float32)
    colour = [jnp.zeros((8, LANES), jnp.float32) for _ in range(3)]
    entering = []
    for s in range(count):
        entering.append(transmit)
        colour = [colour[c] + transmit * agg[s, 1 + c] for c in range(3)]
        transmit = transmit * agg[s, 0]
    picture = colour + [1.0 - transmit]
    behind = -w[0, 3]
    for s in range(count - 1, -1, -1):
        passed = agg[s, 0] * behind
        out[s, 0] = entering[s]
        out[s, 1] = entering[s] * passed
        for j in range(2):
            out[s, 2 + j] = picture[2 * (s % 2) + j]
        glow = w[0, 0] * agg[s, 1] + w[0, 1] * agg[s, 2] + w[0, 2] * agg[s, 3]
        behind = glow + passed


def pixel_grads(got, absorb_part, emit_part, w, v, t, tiles, bands, slabs):
    lanes = pl.ds(t * LANES, LANES)
    owners = [(v * bands + b) * tiles + t for b in range(bands)]
    front = jnp.concatenate([got[n, 0] for n in owners], axis=0)
    passed = jnp.concatenate([got[n, 1] for n in owners], axis=0)
    weight = [front * w[v, c, :, lanes] for c in range(3)]
    for k in range(slabs):
        emit = emit_part[v, k, t]
        parts = [emit * weight[c] for c in range(3)]
        parts.append(front * absorb_part[v, k, t] - passed)
        yield k, parts


def edge_kernel(offs, vids, got, absorb_part, emit_part, w, low, high, half, shifted):
    views, channels, rows, cols = w.shape
    slabs = low.shape[1]
    tiles = cols // LANES
    bands = rows // 8
    edge = jnp.zeros((8, LANES), jnp.float32)
    for n in range(got.shape[0]):
        half[n] = got[n, 2:4]
    moves = [[offs[k, vids[v]] for k in range(slabs)] for v in range(views)]
    for t in range(tiles):
        lanes = pl.ds(t * LANES, LANES)
        for v in range(views):
            grads = pixel_grads(got, absorb_part, emit_part, w, v, t, tiles, bands, slabs)
            for k, parts in grads:
                for c in range(channels):
                    shifted[v, k, c, t, 0:8, :] = edge
                    shifted[v, k, c, t, 8 : 8 + rows, :] = parts[c]
                    shifted[v, k, c, t, 8 + rows : 16 + rows, :] = edge
        for k in range(slabs):
            for c in range(channels):

                def total(start):
                    return sum(
                        shifted[v, k, c, t, pl.ds(start + moves[v][k], 4), :]
                        for v in range(views)
                    )

                low[c, k, :, lanes] = total(4)
                high[c, k, :, lanes] = total(8 + rows)


def main_kernel(offs, vids, got, absorb_part, emit_part, w, main, shifted):
    views, channels, rows, cols = w.shape
    slabs = main.shape[1]
    tiles = cols // LANES
    bands = rows // 8
    edge = jnp.zeros((4, LANES), jnp.float32)
    moves = [[offs[k, vids[v]] for k in range(slabs)] for v in range(views)]
    for t in range(tiles):
        lanes = pl.ds(t * LANES, LANES)
        for v in range(views):
            grads = pixel_grads(got, absorb_part, emit_part, w, v, t, tiles, bands, slabs)
            for k, parts in grads:
                for c in range(channels):
                    shifted[v, k, c, t, 4:8, :] = edge
                    shifted[v, k, c, t, 8 : 8 + rows, :] = parts[c]
                    shifted[v, k, c, t, 8 + rows : 12 + rows, :] = edge
        for k in range(slabs):
            for c in range(channels):
                main[c, k, :, lanes] = sum(
                    shifted[v, k, c, t, pl.ds(8 + moves[v][k], rows), :] for v in range(views)
                )


def join_kernel(place, main, low, high, mine, theirs, out, image):
    rows = main.shape[2]
    views, channels, _, cols = image.shape
    tiles = cols // LANES
    bands = rows // 8
    out[:, :, 0:4, :] = main[:, :, 0:4, :] + low[...]
    out[:, :, 4 : rows - 4, :] = main[:, :, 4 : rows - 4, :]
    out[:, :, rows - 4 :, :] = main[:, :, rows - 4 :, :] + high[...]
    first = 2 * (place[0] % 2)
    for v in range(views):
        for b in range(bands):
            for t in range(tiles):
                n = (v * bands + b) * tiles + t
                for j in range(2):
                    image[v, first + j, 8 * b : 8 * b + 8, t * LANES : (t + 1) * LANES] = mine[n, j]
                    image[v, 2 - first + j, 8 * b : 8 * b + 8, t * LANES : (t + 1) * LANES] = theirs[
                        n, j
                    ]


def on_chip(x):
    return pltpu.with_memory_space_constraint(x, pltpu.VMEM)


def on_device(volume, offsets, view_ids, weights):
    channels, slabs, rows, cols = volume.shape
    views = weights.shape[0]
    count = lax.axis_size("depth")
    strips = lax.axis_size("lat")
    tiles, bands = cols // LANES, rows // 8
    depth_total = slabs * count
    up = [(i, i + 1) for i in range(strips - 1)]
    down = [(i + 1, i) for i in range(strips - 1)]
    pair = [(i, i ^ 1) for i in range(count)]
    f32 = lambda *shape: jax.ShapeDtypeStruct(shape, jnp.float32)
    kept = lambda *shape: pltpu.VMEM(shape, jnp.float32)
    table = offsets.T
    place = lax.axis_index("depth").reshape(1).astype(jnp.int32)
    w = on_chip(weights)

    low = lax.ppermute(volume[:, :, rows - HALO :], "lat", up)
    high = lax.ppermute(volume[:, :, :HALO], "lat", down)
    agg, ext = pl.pallas_call(
        lambda *refs: slab_kernel(depth_total, *refs),
        out_shape=(kept(count, 4, 8, LANES), kept(channels, slabs, tiles, rows + 16, LANES)),
        in_specs=[SMEM, SMEM, VMEM, VMEM, VMEM],
        out_specs=(VMEM, VMEM),
        name="slab",
    )(table, view_ids, on_chip(volume), on_chip(low), on_chip(high))

    agg = lax.all_to_all(agg, "depth", 0, 0, tiled=True)
    absorb_part, emit_part = pl.pallas_call(
        lambda *refs: local_kernel(depth_total, *refs),
        out_shape=(
            kept(views, slabs, tiles, rows, LANES),
            kept(views, slabs, tiles, rows, LANES),
        ),
        in_specs=[SMEM, SMEM, VMEM, VMEM],
        out_specs=(VMEM, VMEM),
        name="local",
    )(table, view_ids, on_chip(ext), w)
    sent = pl.pallas_call(
        scan_kernel,
        out_shape=kept(count, 4, 8, LANES),
        grid_spec=pltpu.PrefetchScalarGridSpec(
            num_scalar_prefetch=1,
            grid=(1,),
            in_specs=[
                VMEM,
                pl.BlockSpec(
                    (1, 4, 8, LANES),
                    lambda i, z: (z[0] // (bands * tiles), 0, (z[0] // tiles) % bands, z[0] % tiles),
                ),
            ],
            out_specs=VMEM,
        ),
        name="scan",
    )(place, on_chip(agg), weights)
    got = on_chip(lax.all_to_all(sent, "depth", 0, 0, tiled=True))

    to_low, to_high, mine = pl.pallas_call(
        edge_kernel,
        out_shape=(
            kept(channels, slabs, HALO, cols),
            kept(channels, slabs, HALO, cols),
            kept(count, 2, 8, LANES),
        ),
        in_specs=[SMEM, SMEM, VMEM, VMEM, VMEM, VMEM],
        out_specs=(VMEM, VMEM, VMEM),
        scratch_shapes=[
            pltpu.VMEM((views, slabs, channels, tiles, rows + 16, LANES), jnp.float32)
        ],
        name="edge",
    )(table, view_ids, got, on_chip(absorb_part), on_chip(emit_part), w)
    from_low = lax.ppermute(to_high, "lat", up)
    from_high = lax.ppermute(to_low, "lat", down)
    theirs = lax.ppermute(mine, "depth", pair)
    main = pl.pallas_call(
        main_kernel,
        out_shape=kept(channels, slabs, rows, cols),
        in_specs=[SMEM, SMEM, VMEM, VMEM, VMEM, VMEM],
        out_specs=VMEM,
        scratch_shapes=[
            pltpu.VMEM((views, slabs, channels, tiles, rows + 16, LANES), jnp.float32)
        ],
        name="main",
    )(table, view_ids, got, on_chip(absorb_part), on_chip(emit_part), w)
    grad_out, image_out = pl.pallas_call(
        join_kernel,
        out_shape=(f32(channels, slabs, rows, cols), f32(views, channels, rows, cols)),
        in_specs=[SMEM, VMEM, VMEM, VMEM, VMEM, VMEM],
        out_specs=(VMEM, VMEM),
        name="join",
    )(place, on_chip(main), on_chip(from_low), on_chip(from_high), on_chip(mine), on_chip(theirs))
    return (image_out, grad_out)


def solution(mesh):
    in_specs = (P(None, "depth", "lat", None), P(None, "depth"), P(), P(None, None, "lat", None))
    out_specs = (P(None, None, "lat", None), P(None, "depth", "lat", None))
    return jax.shard_map(
        on_device, mesh=mesh, in_specs=in_specs, out_specs=out_specs, check_vma=False
    )
```

time: 96 us -> 87.6 us (0.912)
  the two profiles are of different devices: /device:TPU:19 before, /device:TPU:38 now
where the time goes in v2:
time: 87.6 us; the launch traced here: 87 us
  starting transfers between devices  39.3 us (45%)
  waiting for transfers between devices  39.1 us (45%)
  Pallas kernels  6.79 us (8%)
  local copies, waits for them, and re-layouts  1.15 us (1%)
    all_to_all x1, starting transfers between devices, on_device(): agg = lax.all_to_all(agg, 'depth', 0, 0, tiled=True)  15.2 us
    all_to_all x1, waiting for transfers between devices, on_device(): agg = lax.all_to_all(agg, 'depth', 0, 0, tiled=True)  14.6 us
    all_to_all x1, waiting for transfers between devices, on_device(): got = on_chip(lax.all_to_all(sent, 'depth', 0, 0, tiled=True))  14 us
    ppermute x1, starting transfers between devices, on_device(): from_high = lax.ppermute(to_low, 'lat', down)  8.19 us
    ppermute x1, waiting for transfers between devices, on_device(): low = lax.ppermute(volume[:, :, rows - HALO:], 'lat', up)  5.9 us
    all_to_all x1, starting transfers between devices, on_device(): got = on_chip(lax.all_to_all(sent, 'depth', 0, 0, tiled=True))  5.48 us
    ppermute x1, starting transfers between devices, on_device(): high = lax.ppermute(volume[:, :, :HALO], 'lat', down)  4.63 us
    ppermute x1, waiting for transfers between devices, on_device(): theirs = lax.ppermute(mine, 'depth', pair)  3.96 us
  transfers between devices with their start and end apart: 7, of which 5 were waited for; matrix products, arithmetic and copies ran while one was open for 0% of the time, Pallas kernels for 2%

profile of v2, /device:TPU:38, one launch (start us, length us, event | category | flops | bytes accessed | tf_op | source)
XLA Modules:
  0.0 87.0 jit_solution(1097346357064326466)
XLA Ops:
  0.6 0.0 copy-start.1
  0.6 1.1 %fusion = (f32[4,4,4,512]{3,2,1,0:T(4,128)S(1)}, f32[4,4,4,512]{3,2,1,0:T(4,128)S(1)}) fusion(f32[4,4,16,512]{3,2,1,0:T(8,128)} %refs_2_.1), kind=kLoop, calls=%fused_computation | loop fusion | bytes 524288 | tf_op jit(solution)/shard_map/slice | solution.py:199
  1.8 4.6 %collective-permute-start.1 = (f32[4,4,4,512]{3,2,1,0:T(4,128)S(1)}, f32[4,4,4,512]{3,2,1,0:T(4,128)S(1)}, u32[]{:S(2)}, u32[]{:S(2)}) collective-permute-start(f32[4,4,4,512]{3,2,1,0:T(4,128)S(1)} %get-tuple-element.20), channel_id=1, source_target_pairs={{1,0},{2,1},{3,2},{4,3},{5,4},{6,5},{7,6},{8,7},{9,8},{10,9},{11,1... | collective-permute-start | bytes 393224 | tf_op jit(solution)/shard_map/ppermute | solution.py:199
  6.4 1.9 %collective-permute-start = (f32[4,4,4,512]{3,2,1,0:T(4,128)S(1)}, f32[4,4,4,512]{3,2,1,0:T(4,128)S(1)}, u32[]{:S(2)}, u32[]{:S(2)}) collective-permute-start(f32[4,4,4,512]{3,2,1,0:T(4,128)S(1)} %get-tuple-element.21), channel_id=1, source_target_pairs={{0,1},{1,2},{2,3},{3,4},{4,5},{5,6},{6,7},{7,8},{8,9},{9,10},{10,1... | collective-permute-start | bytes 393224 | tf_op jit(solution)/shard_map/ppermute | solution.py:198
  8.3 0.6 collective-permute-done.1.refs_4_
  8.9 5.9 %collective-permute-done.refs_3_ = f32[4,4,4,512]{3,2,1,0:T(4,128)S(1)} collective-permute-done((f32[4,4,4,512]{3,2,1,0:T(4,128)S(1)}, f32[4,4,4,512]{3,2,1,0:T(4,128)S(1)}, u32[]{:S(2)}, u32[]{:S(2)}) %collective-permute-start) | collective-permute-done | bytes 131104 | tf_op jit(solution)/shard_map/ppermute | solution.py:198
  14.8 0.0 copy-done.1
  14.8 1.6 %slab.1 = (f32[16,4,8,128]{3,2,1,0:T(8,128)}, f32[4,4,4,32,128]{4,3,2,1,0:T(8,128)S(1)}) custom-call(s32[4,8]{1,0:T(4,128)} %bitcast.2, s32[2]{0:T(128)} %vids.3, f32[4,4,16,512]{3,2,1,0:T(8,128)S(1)} %copy-done.1, f32[4,4,4,512]{3,2,1,0:T(4,128)S(1)} %collective-permute-done.refs_3_, f32[4,4,4,512]{3,2,1,0:T(4,128)S(1)} %collective-permute-done.1.refs_4_), custom_call_target="tpu_custom_call" | custom-call | tf_op jit(solution)/shard_map/slab/pallas_call | solution.py:200
  16.4 15.2 %all-to-all-start = ((f32[16,4,8,128]{3,2,1,0:T(8,128)}), f32[16,4,8,128]{3,2,1,0:T(8,128)S(1)}, u32[]{:S(2)}, u32[]{:S(2)}) async-start(f32[16,4,8,128]{3,2,1,0:T(8,128)} %get-tuple-element.11), calls=%async_computation | async-start | bytes 524288 | tf_op jit(solution)/shard_map/all_to_all | solution.py:208
  31.6 14.6 %all-to-all-done.agg = f32[16,4,8,128]{3,2,1,0:T(8,128)S(1)} async-done(((f32[16,4,8,128]{3,2,1,0:T(8,128)}), f32[16,4,8,128]{3,2,1,0:T(8,128)S(1)}, u32[]{:S(2)}, u32[]{:S(2)}) %all-to-all-start) | async-done | bytes 262176 | tf_op jit(solution)/shard_map/all_to_all | solution.py:208
  46.2 1.5 %scan.1 = f32[16,4,8,128]{3,2,1,0:T(8,128)} custom-call(s32[1]{0:T(128)} %bitcast.place, f32[16,4,8,128]{3,2,1,0:T(8,128)S(1)} %all-to-all-done.agg, f32[2,4,16,512]{3,2,1,0:T(8,128)} %w.5), custom_call_target="tpu_custom_call" | custom-call | tf_op jit(solution)/shard_map/scan/pallas_call | solution.py:219
  47.7 0.0 copy-start
  47.7 5.5 %all-to-all-start.1 = ((f32[16,4,8,128]{3,2,1,0:T(8,128)}), f32[16,4,8,128]{3,2,1,0:T(8,128)S(1)}, u32[]{:S(2)}, u32[]{:S(2)}) async-start(f32[16,4,8,128]{3,2,1,0:T(8,128)} %scan.1), calls=%async_computation.1 | async-start | bytes 524288 | tf_op jit(solution)/shard_map/all_to_all | solution.py:236
  53.2 0.0 copy-done
  53.2 0.9 local.1
  54.0 14.0 %all-to-all-done.1.got = f32[16,4,8,128]{3,2,1,0:T(8,128)S(1)} async-done(((f32[16,4,8,128]{3,2,1,0:T(8,128)}), f32[16,4,8,128]{3,2,1,0:T(8,128)S(1)}, u32[]{:S(2)}, u32[]{:S(2)}) %all-to-all-start.1) | async-done | bytes 262176 | tf_op jit(solution)/shard_map/all_to_all | solution.py:236
  68.1 0.9 %edge.1 = (f32[4,4,4,512]{3,2,1,0:T(4,128)S(1)}, f32[4,4,4,512]{3,2,1,0:T(4,128)S(1)}, f32[16,2,8,128]{3,2,1,0:T(8,128)S(1)}) custom-call(s32[4,8]{1,0:T(4,128)} %bitcast.4, s32[2]{0:T(128)} %vids.3, f32[16,4,8,128]{3,2,1,0:T(8,128)S(1)} %all-to-all-done.1.got, f32[2,4,4,16,128]{4,3,2,1,0:T(8,128)S(1)} %get-tuple-element.13.absorb_part, ...), custom_call_target="tpu_custom_call" | custom-call | tf_op jit(solution)/shard_map/edge/pallas_call | solution.py:238
  69.0 1.9 %collective-permute-start.2 = (f32[4,4,4,512]{3,2,1,0:T(4,128)S(1)}, f32[4,4,4,512]{3,2,1,0:T(4,128)S(1)}, u32[]{:S(2)}, u32[]{:S(2)}) collective-permute-start(f32[4,4,4,512]{3,2,1,0:T(4,128)S(1)} %get-tuple-element.15), channel_id=1, source_target_pairs={{0,1},{1,2},{2,3},{3,4},{4,5},{5,6},{6,7},{7,8},{8,9},{9,10},{10,1... | collective-permute-start | bytes 393224 | tf_op jit(solution)/shard_map/ppermute | solution.py:252
  71.0 8.2 %collective-permute-start.3 = (f32[4,4,4,512]{3,2,1,0:T(4,128)S(1)}, f32[4,4,4,512]{3,2,1,0:T(4,128)S(1)}, u32[]{:S(2)}, u32[]{:S(2)}) collective-permute-start(f32[4,4,4,512]{3,2,1,0:T(4,128)S(1)} %get-tuple-element.16), channel_id=1, source_target_pairs={{1,0},{2,1},{3,2},{4,3},{5,4},{6,5},{7,6},{8,7},{9,8},{10,9},{11,1... | collective-permute-start | bytes 393224 | tf_op jit(solution)/shard_map/ppermute | solution.py:253
  79.2 1.9 %collective-permute-start.4 = (f32[16,2,8,128]{3,2,1,0:T(8,128)S(1)}, f32[16,2,8,128]{3,2,1,0:T(8,128)S(1)}, u32[]{:S(2)}, u32[]{:S(2)}) collective-permute-start(f32[16,2,8,128]{3,2,1,0:T(8,128)S(1)} %get-tuple-element.17.mine), channel_id=1, source_target_pairs={{0,32},{32,0},{64,96},{96,64},{128,160},{160,128},{192,224},{224,1... | collective-permute-start | bytes 393224 | tf_op jit(solution)/shard_map/ppermute | solution.py:254
  81.1 0.9 %main.1 = f32[4,4,16,512]{3,2,1,0:T(8,128)S(1)} custom-call(s32[4,8]{1,0:T(4,128)} %bitcast.5, s32[2]{0:T(128)} %vids.3, f32[16,4,8,128]{3,2,1,0:T(8,128)S(1)} %all-to-all-done.1.got, f32[2,4,4,16,128]{4,3,2,1,0:T(8,128)S(1)} %get-tuple-element.13.absorb_part, f32[2,4,4,16,128]{4,3,2,1,0:T(8,128)S(1)} %get-tuple-element.14.emit_part, ...), custom_call_target="tpu_custom_call" | custom-call | tf_op jit(solution)/shard_map/main/pallas_call | solution.py:255
  82.0 0.0 collective-permute-done.2.low
  82.0 0.0 collective-permute-done.3.high
  82.1 4.0 %collective-permute-done.4.theirs = f32[16,2,8,128]{3,2,1,0:T(8,128)S(1)} collective-permute-done((f32[16,2,8,128]{3,2,1,0:T(8,128)S(1)}, f32[16,2,8,128]{3,2,1,0:T(8,128)S(1)}, u32[]{:S(2)}, u32[]{:S(2)}) %collective-permute-start.4) | collective-permute-done | bytes 131104 | tf_op jit(solution)/shard_map/ppermute | solution.py:254
  86.0 1.0 %join.1 = (f32[4,4,16,512]{3,2,1,0:T(8,128)}, f32[2,4,16,512]{3,2,1,0:T(8,128)}) custom-call(s32[1]{0:T(128)} %bitcast.place, f32[4,4,16,512]{3,2,1,0:T(8,128)S(1)} %main.1, f32[4,4,4,512]{3,2,1,0:T(4,128)S(1)} %collective-permute-done.2.low, f32[4,4,4,512]{3,2,1,0:T(4,128)S(1)} %collective-permute-done.3.high, ...), custom_call_target="tpu_custom_call" | custom-call | tf_op jit(solution)/shard_map/join/pallas_call | solution.py:265
Async XLA Ops:
  0.6 14.2 %copy-start.1 = (f32[4,4,16,512]{3,2,1,0:T(8,128)S(1)}, f32[4,4,16,512]{3,2,1,0:T(8,128)}, u32[]{:S(2)}) copy-start(f32[4,4,16,512]{3,2,1,0:T(8,128)} %refs_2_.1) | copy-start | bytes 1572868
  1.8 7.1 %collective-permute-start.1 = (f32[4,4,4,512]{3,2,1,0:T(4,128)S(1)}, f32[4,4,4,512]{3,2,1,0:T(4,128)S(1)}, u32[]{:S(2)}, u32[]{:S(2)}) collective-permute-start(f32[4,4,4,512]{3,2,1,0:T(4,128)S(1)} %get-tuple-element.20), channel_id=1, source_target_pairs={{1,0},{2,1},{3,2},{4,3},{5,4},{6,5},{7,6},{8,7},{9,8},{10,9},{11,1... | collective-permute-start | bytes 393224 | tf_op jit(solution)/shard_map/ppermute | solution.py:199
  6.4 8.4 %collective-permute-start = (f32[4,4,4,512]{3,2,1,0:T(4,128)S(1)}, f32[4,4,4,512]{3,2,1,0:T(4,128)S(1)}, u32[]{:S(2)}, u32[]{:S(2)}) collective-permute-start(f32[4,4,4,512]{3,2,1,0:T(4,128)S(1)} %get-tuple-element.21), channel_id=1, source_target_pairs={{0,1},{1,2},{2,3},{3,4},{4,5},{5,6},{6,7},{7,8},{8,9},{9,10},{10,1... | collective-permute-start | bytes 393224 | tf_op jit(solution)/shard_map/ppermute | solution.py:198
  16.4 29.8 %all-to-all-start = ((f32[16,4,8,128]{3,2,1,0:T(8,128)}), f32[16,4,8,128]{3,2,1,0:T(8,128)S(1)}, u32[]{:S(2)}, u32[]{:S(2)}) async-start(f32[16,4,8,128]{3,2,1,0:T(8,128)} %get-tuple-element.11), calls=%async_computation | async-start | bytes 524288 | tf_op jit(solution)/shard_map/all_to_all | solution.py:208
  47.7 5.5 %copy-start = (f32[2,4,16,512]{3,2,1,0:T(8,128)S(1)}, f32[2,4,16,512]{3,2,1,0:T(8,128)}, u32[]{:S(2)}) copy-start(f32[2,4,16,512]{3,2,1,0:T(8,128)} %w.5) | copy-start | bytes 786436
  47.7 20.4 %all-to-all-start.1 = ((f32[16,4,8,128]{3,2,1,0:T(8,128)}), f32[16,4,8,128]{3,2,1,0:T(8,128)S(1)}, u32[]{:S(2)}, u32[]{:S(2)}) async-start(f32[16,4,8,128]{3,2,1,0:T(8,128)} %scan.1), calls=%async_computation.1 | async-start | bytes 524288 | tf_op jit(solution)/shard_map/all_to_all | solution.py:236
  69.0 13.0 %collective-permute-start.2 = (f32[4,4,4,512]{3,2,1,0:T(4,128)S(1)}, f32[4,4,4,512]{3,2,1,0:T(4,128)S(1)}, u32[]{:S(2)}, u32[]{:S(2)}) collective-permute-start(f32[4,4,4,512]{3,2,1,0:T(4,128)S(1)} %get-tuple-element.15), channel_id=1, source_target_pairs={{0,1},{1,2},{2,3},{3,4},{4,5},{5,6},{6,7},{7,8},{8,9},{9,10},{10,1... | collective-permute-start | bytes 393224 | tf_op jit(solution)/shard_map/ppermute | solution.py:252
  71.0 11.1 %collective-permute-start.3 = (f32[4,4,4,512]{3,2,1,0:T(4,128)S(1)}, f32[4,4,4,512]{3,2,1,0:T(4,128)S(1)}, u32[]{:S(2)}, u32[]{:S(2)}) collective-permute-start(f32[4,4,4,512]{3,2,1,0:T(4,128)S(1)} %get-tuple-element.16), channel_id=1, source_target_pairs={{1,0},{2,1},{3,2},{4,3},{5,4},{6,5},{7,6},{8,7},{9,8},{10,9},{11,1... | collective-permute-start | bytes 393224 | tf_op jit(solution)/shard_map/ppermute | solution.py:253
  79.2 6.9 %collective-permute-start.4 = (f32[16,2,8,128]{3,2,1,0:T(8,128)S(1)}, f32[16,2,8,128]{3,2,1,0:T(8,128)S(1)}, u32[]{:S(2)}, u32[]{:S(2)}) collective-permute-start(f32[16,2,8,128]{3,2,1,0:T(8,128)S(1)} %get-tuple-element.17.mine), channel_id=1, source_target_pairs={{0,32},{32,0},{64,96},{96,64},{128,160},{160,128},{192,224},{224,1... | collective-permute-start | bytes 393224 | tf_op jit(solution)/shard_map/ppermute | solution.py:254

commit v3 on v2

--- a/solution.py
+++ b/solution.py
@@ -35,10 +35,10 @@
                 colour = [colour[c] + seen * part[c] for c in range(3)]
                 transmit = transmit * keep
             for b in range(bands):
-                owner = (v * bands + b) * tiles + t
-                agg[owner, 0] = transmit[8 * b : 8 * b + 8]
+                owner = v * bands + b
+                agg[owner, 0, t] = transmit[8 * b : 8 * b + 8]
                 for c in range(3):
-                    agg[owner, 1 + c] = colour[c][8 * b : 8 * b + 8]
+                    agg[owner, 1 + c, t] = colour[c][8 * b : 8 * b + 8]
 
 
 def local_kernel(depth_total, offs, vids, ext, w, absorb_part, emit_part):
@@ -67,32 +67,70 @@
                 behind = alphas[k] * glows[k] + keeps[k] * behind
 
 
-def scan_kernel(place, agg, w, out):
-    count = agg.shape[0]
-    transmit = jnp.ones((8, LANES), jnp.float32)
-    colour = [jnp.zeros((8, LANES), jnp.float32) for _ in range(3)]
-    entering = []
-    for s in range(count):
-        entering.append(transmit)
-        colour = [colour[c] + transmit * agg[s, 1 + c] for c in range(3)]
-        transmit = transmit * agg[s, 0]
-    picture = colour + [1.0 - transmit]
-    behind = -w[0, 3]
-    for s in range(count - 1, -1, -1):
-        passed = agg[s, 0] * behind
-        out[s, 0] = entering[s]
-        out[s, 1] = entering[s] * passed
-        for j in range(2):
-            out[s, 2 + j] = picture[2 * (s % 2) + j]
-        glow = w[0, 0] * agg[s, 1] + w[0, 1] * agg[s, 2] + w[0, 2] * agg[s, 3]
-        behind = glow + passed
+def seat(place, members):
+    mine, member = lax.div(place[0], members), lax.rem(place[0], members)
+    turned = (mine == 1) | (mine == 2)
+    order = [jnp.where(turned, members - 1 - j, j) for j in range(members)]
+    return mine, jnp.where(turned, members - 1 - member, member), order
+
+
+def group_kernel(place, agg, out):
+    members, _, tiles = agg.shape[:3]
+    _, _, order = seat(place, members)
+    for t in range(tiles):
+        transmit = agg[order[0], 0, t]
+        colour = [agg[order[0], 1 + c, t] for c in range(3)]
+        for j in range(1, members):
+            colour = [colour[c] + transmit * agg[order[j], 1 + c, t] for c in range(3)]
+            transmit = transmit * agg[order[j], 0, t]
+        for n in range(out.shape[0]):
+            out[n, 0, t] = transmit
+            for c in range(3):
+                out[n, 1 + c, t] = colour[c]
+
+
+def scan_kernel(place, agg, groups, w, out):
+    members, _, tiles = agg.shape[:3]
+    mine, owner, order = seat(place, members)
+    bands = w.shape[2] // 8
+    view, band = lax.div(owner, bands), lax.rem(owner, bands)
+    rows = pl.ds(pl.multiple_of(8 * band, 8), 8)
+    for t in range(tiles):
+        lanes = pl.ds(t * LANES, LANES)
+        weight = [w[view, c, rows, lanes] for c in range(4)]
+        transmit = jnp.ones((8, LANES), jnp.float32)
+        colour = [jnp.zeros((8, LANES), jnp.float32) for _ in range(3)]
+        front = transmit
+        count = groups.shape[0]
+        for g in range(count):
+            front = jnp.where(mine == g, transmit, front)
+            colour = [colour[c] + transmit * groups[g, 1 + c, t] for c in range(3)]
+            transmit = transmit * groups[g, 0, t]
+        picture = colour + [1.0 - transmit]
+        behind = -weight[3]
+        enter = behind
+        for g in range(count - 1, 0, -1):
+            glow = sum(weight[c] * groups[g, 1 + c, t] for c in range(3))
+            behind = glow + groups[g, 0, t] * behind
+            enter = jnp.where(mine == g - 1, behind, enter)
+        fronts = []
+        for j in range(members):
+            fronts.append(front)
+            front = front * agg[order[j], 0, t]
+        for j in range(members - 1, -1, -1):
+            passed = agg[order[j], 0, t] * enter
+            out[order[j], 0, t] = fronts[j]
+            out[order[j], 1, t] = fronts[j] * passed
+            for c in range(4):
+                out[order[j], 2 + c, t] = picture[c]
+            enter = passed + sum(weight[c] * agg[order[j], 1 + c, t] for c in range(3))
 
 
 def pixel_grads(got, absorb_part, emit_part, w, v, t, tiles, bands, slabs):
     lanes = pl.ds(t * LANES, LANES)
-    owners = [(v * bands + b) * tiles + t for b in range(bands)]
-    front = jnp.concatenate([got[n, 0] for n in owners], axis=0)
-    passed = jnp.concatenate([got[n, 1] for n in owners], axis=0)
+    owners = [v * bands + b for b in range(bands)]
+    front = jnp.concatenate([got[n, 0, t] for n in owners], axis=0)
+    passed = jnp.concatenate([got[n, 1, t] for n in owners], axis=0)
     weight = [front * w[v, c, :, lanes] for c in range(3)]
     for k in range(slabs):
         emit = emit_part[v, k, t]
@@ -101,14 +139,12 @@
         yield k, parts
 
 
-def edge_kernel(offs, vids, got, absorb_part, emit_part, w, low, high, half, shifted):
+def edge_kernel(offs, vids, got, absorb_part, emit_part, w, low, high, shifted):
     views, channels, rows, cols = w.shape
     slabs = low.shape[1]
     tiles = cols // LANES
     bands = rows // 8
     edge = jnp.zeros((8, LANES), jnp.float32)
-    for n in range(got.shape[0]):
-        half[n] = got[n, 2:4]
     moves = [[offs[k, vids[v]] for k in range(slabs)] for v in range(views)]
     for t in range(tiles):
         lanes = pl.ds(t * LANES, LANES)
@@ -155,23 +191,19 @@
                 )
 
 
-def join_kernel(place, main, low, high, mine, theirs, out, image):
+def join_kernel(main, low, high, got, out, image):
     rows = main.shape[2]
     views, channels, _, cols = image.shape
-    tiles = cols // LANES
     bands = rows // 8
     out[:, :, 0:4, :] = main[:, :, 0:4, :] + low[...]
     out[:, :, 4 : rows - 4, :] = main[:, :, 4 : rows - 4, :]
     out[:, :, rows - 4 :, :] = main[:, :, rows - 4 :, :] + high[...]
-    first = 2 * (place[0] % 2)
     for v in range(views):
         for b in range(bands):
-            for t in range(tiles):
-                n = (v * bands + b) * tiles + t
-                for j in range(2):
-                    image[v, first + j, 8 * b : 8 * b + 8, t * LANES : (t + 1) * LANES] = mine[n, j]
-                    image[v, 2 - first + j, 8 * b : 8 * b + 8, t * LANES : (t + 1) * LANES] = theirs[
-                        n, j
+            for t in range(cols // LANES):
+                for c in range(channels):
+                    image[v, c, 8 * b : 8 * b + 8, t * LANES : (t + 1) * LANES] = got[
+                        v * bands + b, 2 + c, t
                     ]
 
 
@@ -186,26 +218,42 @@
     strips = lax.axis_size("lat")
     tiles, bands = cols // LANES, rows // 8
     depth_total = slabs * count
+    size = views * bands
+    near = [[size * g + i for i in range(size)] for g in range(count // size)]
+    near = [row[::-1] if g in (1, 2) else row for g, row in enumerate(near)]
+    far = [[row[i] for row in near] for i in range(size)]
     up = [(i, i + 1) for i in range(strips - 1)]
     down = [(i + 1, i) for i in range(strips - 1)]
-    pair = [(i, i ^ 1) for i in range(count)]
     f32 = lambda *shape: jax.ShapeDtypeStruct(shape, jnp.float32)
     kept = lambda *shape: pltpu.VMEM(shape, jnp.float32)
     table = offsets.T
     place = lax.axis_index("depth").reshape(1).astype(jnp.int32)
     w = on_chip(weights)
 
+    def swap(x, groups):
+        return lax.all_to_all(x, "depth", 0, 0, tiled=True, axis_index_groups=groups)
+
     low = lax.ppermute(volume[:, :, rows - HALO :], "lat", up)
     high = lax.ppermute(volume[:, :, :HALO], "lat", down)
     agg, ext = pl.pallas_call(
         lambda *refs: slab_kernel(depth_total, *refs),
-        out_shape=(kept(count, 4, 8, LANES), kept(channels, slabs, tiles, rows + 16, LANES)),
+        out_shape=(
+            kept(size, 4, tiles, 8, LANES),
+            kept(channels, slabs, tiles, rows + 16, LANES),
+        ),
         in_specs=[SMEM, SMEM, VMEM, VMEM, VMEM],
         out_specs=(VMEM, VMEM),
         name="slab",
     )(table, view_ids, on_chip(volume), on_chip(low), on_chip(high))
-
-    agg = lax.all_to_all(agg, "depth", 0, 0, tiled=True)
+    agg = on_chip(swap(agg, near))
+    grouped = pl.pallas_call(
+        group_kernel,
+        out_shape=kept(count // size, 4, tiles, 8, LANES),
+        in_specs=[SMEM, VMEM],
+        out_specs=VMEM,
+        name="group",
+    )(place, agg)
+    groups = on_chip(swap(grouped, far))
     absorb_part, emit_part = pl.pallas_call(
         lambda *refs: local_kernel(depth_total, *refs),
         out_shape=(
@@ -218,32 +266,21 @@
     )(table, view_ids, on_chip(ext), w)
     sent = pl.pallas_call(
         scan_kernel,
-        out_shape=kept(count, 4, 8, LANES),
-        grid_spec=pltpu.PrefetchScalarGridSpec(
-            num_scalar_prefetch=1,
-            grid=(1,),
-            in_specs=[
-                VMEM,
-                pl.BlockSpec(
-                    (1, 4, 8, LANES),
-                    lambda i, z: (z[0] // (bands * tiles), 0, (z[0] // tiles) % bands, z[0] % tiles),
-                ),
-            ],
-            out_specs=VMEM,
-        ),
+        out_shape=kept(size, 6, tiles, 8, LANES),
+        in_specs=[SMEM, VMEM, VMEM, VMEM],
+        out_specs=VMEM,
         name="scan",
-    )(place, on_chip(agg), weights)
-    got = on_chip(lax.all_to_all(sent, "depth", 0, 0, tiled=True))
-
-    to_low, to_high, mine = pl.pallas_call(
+    )(place, agg, groups, w)
+    got = on_chip(swap(sent, near))
+
+    to_low, to_high = pl.pallas_call(
         edge_kernel,
         out_shape=(
             kept(channels, slabs, HALO, cols),
             kept(channels, slabs, HALO, cols),
-            kept(count, 2, 8, LANES),
         ),
         in_specs=[SMEM, SMEM, VMEM, VMEM, VMEM, VMEM],
-        out_specs=(VMEM, VMEM, VMEM),
+        out_specs=(VMEM, VMEM),
         scratch_shapes=[
             pltpu.VMEM((views, slabs, channels, tiles, rows + 16, LANES), jnp.float32)
         ],
@@ -251,7 +288,6 @@
     )(table, view_ids, got, on_chip(absorb_part), on_chip(emit_part), w)
     from_low = lax.ppermute(to_high, "lat", up)
     from_high = lax.ppermute(to_low, "lat", down)
-    theirs = lax.ppermute(mine, "depth", pair)
     main = pl.pallas_call(
         main_kernel,
         out_shape=kept(channels, slabs, rows, cols),
@@ -265,10 +301,10 @@
     grad_out, image_out = pl.pallas_call(
         join_kernel,
         out_shape=(f32(channels, slabs, rows, cols), f32(views, channels, rows, cols)),
-        in_specs=[SMEM, VMEM, VMEM, VMEM, VMEM, VMEM],
+        in_specs=[VMEM, VMEM, VMEM, VMEM],
         out_specs=(VMEM, VMEM),
         name="join",
-    )(place, on_chip(main), on_chip(from_low), on_chip(from_high), on_chip(mine), on_chip(theirs))
+    )(on_chip(main), on_chip(from_low), on_chip(from_high), got)
     return (image_out, grad_out)
 
 

time: 87.6 us -> 86.3 us (0.985)
  the two profiles are of different devices: /device:TPU:38 before, /device:TPU:19 now
where the time goes in v3:
time: 86.3 us; the launch traced here: 85.8 us
  starting transfers between devices  34.9 us (40%)
  blocking collectives  21.5 us (25%)
  waiting for transfers between devices  21.4 us (25%)
  Pallas kernels  6.13 us (7%)
  local copies, waits for them, and re-layouts  1.15 us (1%)
    all_to_all x1, blocking collectives, swap(): lax.all_to_all(x, 'depth', 0, 0, tiled=True, axis_index_groups=groups)  21.5 us
    all_to_all x2, starting transfers between devices, swap(): lax.all_to_all(x, 'depth', 0, 0, tiled=True, axis_index_groups=groups)  19.4 us
    all_to_all x2, waiting for transfers between devices, swap(): lax.all_to_all(x, 'depth', 0, 0, tiled=True, axis_index_groups=groups)  16.1 us
    ppermute x1, starting transfers between devices, on_device(): from_low = lax.ppermute(to_high, 'lat', up)  7.95 us
    ppermute x1, waiting for transfers between devices, on_device(): from_high = lax.ppermute(to_low, 'lat', down)  3.4 us
    ppermute x1, starting transfers between devices, on_device(): low = lax.ppermute(volume[:, :, rows - HALO:], 'lat', up)  2.98 us
    ppermute x1, starting transfers between devices, on_device(): high = lax.ppermute(volume[:, :, :HALO], 'lat', down)  2.58 us
    ppermute x1, starting transfers between devices, on_device(): from_high = lax.ppermute(to_low, 'lat', down)  1.92 us
  transfers between devices with their start and end apart: 6, of which 5 were waited for; matrix products, arithmetic and copies ran while one was open for 0% of the time, Pallas kernels for 2%

profile of v3, /device:TPU:19, one launch (start us, length us, event | category | flops | bytes accessed | tf_op | source)
XLA Modules:
  0.0 85.8 jit_solution(18090753284774558320)
XLA Ops:
  0.6 0.0 copy-start.1
  0.6 1.1 %fusion = (f32[4,4,4,512]{3,2,1,0:T(4,128)S(1)}, f32[4,4,4,512]{3,2,1,0:T(4,128)S(1)}) fusion(f32[4,4,16,512]{3,2,1,0:T(8,128)} %refs_2_.1), kind=kLoop, calls=%fused_computation | loop fusion | bytes 524288 | tf_op jit(solution)/shard_map/slice | solution.py:237
  1.8 2.6 %collective-permute-start.1 = (f32[4,4,4,512]{3,2,1,0:T(4,128)S(1)}, f32[4,4,4,512]{3,2,1,0:T(4,128)S(1)}, u32[]{:S(2)}, u32[]{:S(2)}) collective-permute-start(f32[4,4,4,512]{3,2,1,0:T(4,128)S(1)} %get-tuple-element.18), channel_id=1, source_target_pairs={{1,0},{2,1},{3,2},{4,3},{5,4},{6,5},{7,6},{8,7},{9,8},{10,9},{11,1... | collective-permute-start | bytes 393224 | tf_op jit(solution)/shard_map/ppermute | solution.py:237
  4.4 3.0 %collective-permute-start = (f32[4,4,4,512]{3,2,1,0:T(4,128)S(1)}, f32[4,4,4,512]{3,2,1,0:T(4,128)S(1)}, u32[]{:S(2)}, u32[]{:S(2)}) collective-permute-start(f32[4,4,4,512]{3,2,1,0:T(4,128)S(1)} %get-tuple-element.19), channel_id=1, source_target_pairs={{0,1},{1,2},{2,3},{3,4},{4,5},{5,6},{6,7},{7,8},{8,9},{9,10},{10,1... | collective-permute-start | bytes 393224 | tf_op jit(solution)/shard_map/ppermute | solution.py:236
  7.4 0.7 collective-permute-done.1.refs_4_
  8.1 1.2 %collective-permute-done.refs_3_ = f32[4,4,4,512]{3,2,1,0:T(4,128)S(1)} collective-permute-done((f32[4,4,4,512]{3,2,1,0:T(4,128)S(1)}, f32[4,4,4,512]{3,2,1,0:T(4,128)S(1)}, u32[]{:S(2)}, u32[]{:S(2)}) %collective-permute-start) | collective-permute-done | bytes 131104 | tf_op jit(solution)/shard_map/ppermute | solution.py:236
  9.3 0.0 copy-done.1
  9.3 1.6 %slab.1 = (f32[4,4,4,8,128]{4,3,2,1,0:T(8,128)}, f32[4,4,4,32,128]{4,3,2,1,0:T(8,128)S(1)}) custom-call(s32[4,8]{1,0:T(4,128)} %bitcast.2, s32[2]{0:T(128)} %vids.3, f32[4,4,16,512]{3,2,1,0:T(8,128)S(1)} %copy-done.1, f32[4,4,4,512]{3,2,1,0:T(4,128)S(1)} %collective-permute-done.refs_3_, f32[4,4,4,512]{3,2,1,0:T(4,128)S(1)} %collective-permute-done.1.refs_4_), custom_call_target="tpu_custom_call" | custom-call | tf_op jit(solution)/shard_map/slab/pallas_call | solution.py:238
  10.9 5.6 %all-to-all-start = ((f32[4,4,4,8,128]{4,3,2,1,0:T(8,128)}), f32[4,4,4,8,128]{4,3,2,1,0:T(8,128)S(1)}, u32[]{:S(2)}, u32[]{:S(2)}) async-start(f32[4,4,4,8,128]{4,3,2,1,0:T(8,128)} %get-tuple-element.10), calls=%async_computation | async-start | bytes 524288 | tf_op jit(solution)/shard_map/all_to_all | solution.py:234
  16.5 5.7 %all-to-all-done.agg = f32[4,4,4,8,128]{4,3,2,1,0:T(8,128)S(1)} async-done(((f32[4,4,4,8,128]{4,3,2,1,0:T(8,128)}), f32[4,4,4,8,128]{4,3,2,1,0:T(8,128)S(1)}, u32[]{:S(2)}, u32[]{:S(2)}) %all-to-all-start) | async-done | bytes 262176 | tf_op jit(solution)/shard_map/all_to_all | solution.py:234
  22.2 0.0 copy-start
  22.2 21.5 %all_to_all.15.groups = f32[4,4,4,8,128]{4,3,2,1,0:T(8,128)S(1)} all-to-all(f32[4,4,4,8,128]{4,3,2,1,0:T(8,128)S(1)} %group.1), channel_id=1, replica_groups={{0,224,352,384},{32,192,320,416},{64,160,288,448},{96,128,256,480},{1,2..., dimensions={0} | all-to-all | bytes 524288 | tf_op jit(solution)/shard_map/all_to_all | solution.py:234
  43.7 0.0 copy-done
  43.7 0.8 scan.1
  44.6 13.8 %all-to-all-start.2 = ((f32[4,6,4,8,128]{4,3,2,1,0:T(8,128)}), f32[4,6,4,8,128]{4,3,2,1,0:T(8,128)S(1)}, u32[]{:S(2)}, u32[]{:S(2)}) async-start(f32[4,6,4,8,128]{4,3,2,1,0:T(8,128)} %scan.1), calls=%async_computation.2 | async-start | bytes 786432 | tf_op jit(solution)/shard_map/all_to_all | solution.py:234
  58.4 0.9 %local.1 = (f32[2,4,4,16,128]{4,3,2,1,0:T(8,128)S(1)}, f32[2,4,4,16,128]{4,3,2,1,0:T(8,128)S(1)}) custom-call(s32[4,8]{1,0:T(4,128)} %bitcast.3, s32[2]{0:T(128)} %vids.3, f32[4,4,4,32,128]{4,3,2,1,0:T(8,128)S(1)} %get-tuple-element.11.refs_2_, f32[2,4,16,512]{3,2,1,0:T(8,128)S(1)} %copy-done), custom_call_target="tpu_custom_call" | custom-call | tf_op jit(solution)/shard_map/local/pallas_call | solution.py:257
  59.2 10.4 %all-to-all-done.2.got = f32[4,6,4,8,128]{4,3,2,1,0:T(8,128)S(1)} async-done(((f32[4,6,4,8,128]{4,3,2,1,0:T(8,128)}), f32[4,6,4,8,128]{4,3,2,1,0:T(8,128)S(1)}, u32[]{:S(2)}, u32[]{:S(2)}) %all-to-all-start.2) | async-done | bytes 393248 | tf_op jit(solution)/shard_map/all_to_all | solution.py:234
  69.6 0.9 %edge.1 = (f32[4,4,4,512]{3,2,1,0:T(4,128)S(1)}, f32[4,4,4,512]{3,2,1,0:T(4,128)S(1)}) custom-call(s32[4,8]{1,0:T(4,128)} %bitcast.4, s32[2]{0:T(128)} %vids.3, f32[4,6,4,8,128]{4,3,2,1,0:T(8,128)S(1)} %all-to-all-done.2.got, f32[2,4,4,16,128]{4,3,2,1,0:T(8,128)S(1)} %get-tuple-element.12.absorb_part, f32[2,4,4,16,128]{4,3,2,1,0:T(8,128)S(1)} %get-tuple-element.13.emit_part, ...), custom_call_target="tpu_custom_call" | custom-call | tf_op jit(solution)/shard_map/edge/pallas_call | solution.py:276
  70.5 8.0 %collective-permute-start.2 = (f32[4,4,4,512]{3,2,1,0:T(4,128)S(1)}, f32[4,4,4,512]{3,2,1,0:T(4,128)S(1)}, u32[]{:S(2)}, u32[]{:S(2)}) collective-permute-start(f32[4,4,4,512]{3,2,1,0:T(4,128)S(1)} %get-tuple-element.14), channel_id=1, source_target_pairs={{0,1},{1,2},{2,3},{3,4},{4,5},{5,6},{6,7},{7,8},{8,9},{9,10},{10,1... | collective-permute-start | bytes 393224 | tf_op jit(solution)/shard_map/ppermute | solution.py:289
  78.5 1.9 %collective-permute-start.3 = (f32[4,4,4,512]{3,2,1,0:T(4,128)S(1)}, f32[4,4,4,512]{3,2,1,0:T(4,128)S(1)}, u32[]{:S(2)}, u32[]{:S(2)}) collective-permute-start(f32[4,4,4,512]{3,2,1,0:T(4,128)S(1)} %get-tuple-element.15), channel_id=1, source_target_pairs={{1,0},{2,1},{3,2},{4,3},{5,4},{6,5},{7,6},{8,7},{9,8},{10,9},{11,1... | collective-permute-start | bytes 393224 | tf_op jit(solution)/shard_map/ppermute | solution.py:290
  80.4 0.9 %main.1 = f32[4,4,16,512]{3,2,1,0:T(8,128)S(1)} custom-call(s32[4,8]{1,0:T(4,128)} %bitcast.5, s32[2]{0:T(128)} %vids.3, f32[4,6,4,8,128]{4,3,2,1,0:T(8,128)S(1)} %all-to-all-done.2.got, f32[2,4,4,16,128]{4,3,2,1,0:T(8,128)S(1)} %get-tuple-element.12.absorb_part, f32[2,4,4,16,128]{4,3,2,1,0:T(8,128)S(1)} %get-tuple-element.13.emit_part, ...), custom_call_target="tpu_custom_call" | custom-call | tf_op jit(solution)/shard_map/main/pallas_call | solution.py:291
  81.4 0.0 collective-permute-done.2.low
  81.4 3.4 %collective-permute-done.3.high = f32[4,4,4,512]{3,2,1,0:T(4,128)S(1)} collective-permute-done((f32[4,4,4,512]{3,2,1,0:T(4,128)S(1)}, f32[4,4,4,512]{3,2,1,0:T(4,128)S(1)}, u32[]{:S(2)}, u32[]{:S(2)}) %collective-permute-start.3) | collective-permute-done | bytes 131104 | tf_op jit(solution)/shard_map/ppermute | solution.py:290
  84.8 1.0 %join.1 = (f32[4,4,16,512]{3,2,1,0:T(8,128)}, f32[2,4,16,512]{3,2,1,0:T(8,128)}) custom-call(f32[4,4,16,512]{3,2,1,0:T(8,128)S(1)} %main.1, f32[4,4,4,512]{3,2,1,0:T(4,128)S(1)} %collective-permute-done.2.low, f32[4,4,4,512]{3,2,1,0:T(4,128)S(1)} %collective-permute-done.3.high, f32[4,6,4,8,128]{4,3,2,1,0:T(8,128)S(1)} %all-to-all-done.2.got), custom_call_target="tpu_custom_call" | custom-call | tf_op jit(solution)/shard_map/join/pallas_call | solution.py:301
  (1 shorter events, 0.0 us)
Async XLA Ops:
  0.6 8.7 %copy-start.1 = (f32[4,4,16,512]{3,2,1,0:T(8,128)S(1)}, f32[4,4,16,512]{3,2,1,0:T(8,128)}, u32[]{:S(2)}) copy-start(f32[4,4,16,512]{3,2,1,0:T(8,128)} %refs_2_.1) | copy-start | bytes 1572868
  1.8 6.3 %collective-permute-start.1 = (f32[4,4,4,512]{3,2,1,0:T(4,128)S(1)}, f32[4,4,4,512]{3,2,1,0:T(4,128)S(1)}, u32[]{:S(2)}, u32[]{:S(2)}) collective-permute-start(f32[4,4,4,512]{3,2,1,0:T(4,128)S(1)} %get-tuple-element.18), channel_id=1, source_target_pairs={{1,0},{2,1},{3,2},{4,3},{5,4},{6,5},{7,6},{8,7},{9,8},{10,9},{11,1... | collective-permute-start | bytes 393224 | tf_op jit(solution)/shard_map/ppermute | solution.py:237
  4.4 4.9 %collective-permute-start = (f32[4,4,4,512]{3,2,1,0:T(4,128)S(1)}, f32[4,4,4,512]{3,2,1,0:T(4,128)S(1)}, u32[]{:S(2)}, u32[]{:S(2)}) collective-permute-start(f32[4,4,4,512]{3,2,1,0:T(4,128)S(1)} %get-tuple-element.19), channel_id=1, source_target_pairs={{0,1},{1,2},{2,3},{3,4},{4,5},{5,6},{6,7},{7,8},{8,9},{9,10},{10,1... | collective-permute-start | bytes 393224 | tf_op jit(solution)/shard_map/ppermute | solution.py:236
  10.9 11.3 %all-to-all-start = ((f32[4,4,4,8,128]{4,3,2,1,0:T(8,128)}), f32[4,4,4,8,128]{4,3,2,1,0:T(8,128)S(1)}, u32[]{:S(2)}, u32[]{:S(2)}) async-start(f32[4,4,4,8,128]{4,3,2,1,0:T(8,128)} %get-tuple-element.10), calls=%async_computation | async-start | bytes 524288 | tf_op jit(solution)/shard_map/all_to_all | solution.py:234
  22.2 21.5 %copy-start = (f32[2,4,16,512]{3,2,1,0:T(8,128)S(1)}, f32[2,4,16,512]{3,2,1,0:T(8,128)}, u32[]{:S(2)}) copy-start(f32[2,4,16,512]{3,2,1,0:T(8,128)} %w.5) | copy-start | bytes 786436
  44.6 25.1 %all-to-all-start.2 = ((f32[4,6,4,8,128]{4,3,2,1,0:T(8,128)}), f32[4,6,4,8,128]{4,3,2,1,0:T(8,128)S(1)}, u32[]{:S(2)}, u32[]{:S(2)}) async-start(f32[4,6,4,8,128]{4,3,2,1,0:T(8,128)} %scan.1), calls=%async_computation.2 | async-start | bytes 786432 | tf_op jit(solution)/shard_map/all_to_all | solution.py:234
  70.5 10.8 %collective-permute-start.2 = (f32[4,4,4,512]{3,2,1,0:T(4,128)S(1)}, f32[4,4,4,512]{3,2,1,0:T(4,128)S(1)}, u32[]{:S(2)}, u32[]{:S(2)}) collective-permute-start(f32[4,4,4,512]{3,2,1,0:T(4,128)S(1)} %get-tuple-element.14), channel_id=1, source_target_pairs={{0,1},{1,2},{2,3},{3,4},{4,5},{5,6},{6,7},{7,8},{8,9},{9,10},{10,1... | collective-permute-start | bytes 393224 | tf_op jit(solution)/shard_map/ppermute | solution.py:289
  78.5 6.3 %collective-permute-start.3 = (f32[4,4,4,512]{3,2,1,0:T(4,128)S(1)}, f32[4,4,4,512]{3,2,1,0:T(4,128)S(1)}, u32[]{:S(2)}, u32[]{:S(2)}) collective-permute-start(f32[4,4,4,512]{3,2,1,0:T(4,128)S(1)} %get-tuple-element.15), channel_id=1, source_target_pairs={{1,0},{2,1},{3,2},{4,3},{5,4},{6,5},{7,6},{8,7},{9,8},{10,9},{11,1... | collective-permute-start | bytes 393224 | tf_op jit(solution)/shard_map/ppermute | solution.py:290

commit v4 on v3

--- a/solution.py
+++ b/solution.py
@@ -89,7 +89,7 @@
                 out[n, 1 + c, t] = colour[c]
 
 
-def scan_kernel(place, agg, groups, w, out):
+def scan_kernel(place, agg, groups, w, out, shown):
     members, _, tiles = agg.shape[:3]
     mine, owner, order = seat(place, members)
     bands = w.shape[2] // 8
@@ -122,7 +122,7 @@
             out[order[j], 0, t] = fronts[j]
             out[order[j], 1, t] = fronts[j] * passed
             for c in range(4):
-                out[order[j], 2 + c, t] = picture[c]
+                shown[j, c, t] = picture[c]
             enter = passed + sum(weight[c] * agg[order[j], 1 + c, t] for c in range(3))
 
 
@@ -191,7 +191,7 @@
                 )
 
 
-def join_kernel(main, low, high, got, out, image):
+def join_kernel(main, low, high, shown, out, image):
     rows = main.shape[2]
     views, channels, _, cols = image.shape
     bands = rows // 8
@@ -202,8 +202,8 @@
         for b in range(bands):
             for t in range(cols // LANES):
                 for c in range(channels):
-                    image[v, c, 8 * b : 8 * b + 8, t * LANES : (t + 1) * LANES] = got[
-                        v * bands + b, 2 + c, t
+                    image[v, c, 8 * b : 8 * b + 8, t * LANES : (t + 1) * LANES] = shown[
+                        v * bands + b, c, t
                     ]
 
 
@@ -264,14 +264,15 @@
         out_specs=(VMEM, VMEM),
         name="local",
     )(table, view_ids, on_chip(ext), w)
-    sent = pl.pallas_call(
+    sent, shown = pl.pallas_call(
         scan_kernel,
-        out_shape=kept(size, 6, tiles, 8, LANES),
+        out_shape=(kept(size, 2, tiles, 8, LANES), kept(size, 4, tiles, 8, LANES)),
         in_specs=[SMEM, VMEM, VMEM, VMEM],
-        out_specs=VMEM,
+        out_specs=(VMEM, VMEM),
         name="scan",
     )(place, agg, groups, w)
     got = on_chip(swap(sent, near))
+    shown = swap(shown, near)
 
     to_low, to_high = pl.pallas_call(
         edge_kernel,
@@ -304,7 +305,7 @@
         in_specs=[VMEM, VMEM, VMEM, VMEM],
         out_specs=(VMEM, VMEM),
         name="join",
-    )(on_chip(main), on_chip(from_low), on_chip(from_high), got)
+    )(on_chip(main), on_chip(from_low), on_chip(from_high), on_chip(shown))
     return (image_out, grad_out)
 
 

time: 86.3 us -> 85 us (0.985)
  the two profiles are of different devices: /device:TPU:19 before, /device:TPU:59 now
where the time goes in v4:
time: 85 us; the launch traced here: 84.4 us
  blocking collectives  38.4 us (45%)
  starting transfers between devices  23.2 us (27%)
  waiting for transfers between devices  14.9 us (18%)
  Pallas kernels  6.1 us (7%)
  local copies, waits for them, and re-layouts  1.15 us (1%)
    all_to_all x2, blocking collectives, swap(): lax.all_to_all(x, 'depth', 0, 0, tiled=True, axis_index_groups=groups)  38.4 us
    all_to_all x2, starting transfers between devices, swap(): lax.all_to_all(x, 'depth', 0, 0, tiled=True, axis_index_groups=groups)  9.3 us
    all_to_all x2, waiting for transfers between devices, swap(): lax.all_to_all(x, 'depth', 0, 0, tiled=True, axis_index_groups=groups)  7.65 us
    ppermute x1, waiting for transfers between devices, on_device(): from_high = lax.ppermute(to_low, 'lat', down)  5.29 us
    ppermute x1, starting transfers between devices, on_device(): low = lax.ppermute(volume[:, :, rows - HALO:], 'lat', up)  5.09 us
    ppermute x1, starting transfers between devices, on_device(): from_low = lax.ppermute(to_high, 'lat', up)  4.11 us
    ppermute x1, starting transfers between devices, on_device(): high = lax.ppermute(volume[:, :, :HALO], 'lat', down)  2.58 us
    ppermute x1, starting transfers between devices, on_device(): from_high = lax.ppermute(to_low, 'lat', down)  2.14 us
  transfers between devices with their start and end apart: 6, of which 4 were waited for; matrix products, arithmetic and copies ran while one was open for 0% of the time, Pallas kernels for 3%

profile of v4, /device:TPU:59, one launch (start us, length us, event | category | flops | bytes accessed | tf_op | source)
XLA Modules:
  0.0 84.4 jit_solution(4795872600886389868)
XLA Ops:
  0.6 0.0 copy-start.1
  0.6 1.1 %fusion = (f32[4,4,4,512]{3,2,1,0:T(4,128)S(1)}, f32[4,4,4,512]{3,2,1,0:T(4,128)S(1)}) fusion(f32[4,4,16,512]{3,2,1,0:T(8,128)} %refs_2_.1), kind=kLoop, calls=%fused_computation | loop fusion | bytes 524288 | tf_op jit(solution)/shard_map/slice | solution.py:237
  1.8 2.6 %collective-permute-start.1 = (f32[4,4,4,512]{3,2,1,0:T(4,128)S(1)}, f32[4,4,4,512]{3,2,1,0:T(4,128)S(1)}, u32[]{:S(2)}, u32[]{:S(2)}) collective-permute-start(f32[4,4,4,512]{3,2,1,0:T(4,128)S(1)} %get-tuple-element.22), channel_id=1, source_target_pairs={{1,0},{2,1},{3,2},{4,3},{5,4},{6,5},{7,6},{8,7},{9,8},{10,9},{11,1... | collective-permute-start | bytes 393224 | tf_op jit(solution)/shard_map/ppermute | solution.py:237
  4.4 5.1 %collective-permute-start = (f32[4,4,4,512]{3,2,1,0:T(4,128)S(1)}, f32[4,4,4,512]{3,2,1,0:T(4,128)S(1)}, u32[]{:S(2)}, u32[]{:S(2)}) collective-permute-start(f32[4,4,4,512]{3,2,1,0:T(4,128)S(1)} %get-tuple-element.23), channel_id=1, source_target_pairs={{0,1},{1,2},{2,3},{3,4},{4,5},{5,6},{6,7},{7,8},{8,9},{9,10},{10,1... | collective-permute-start | bytes 393224 | tf_op jit(solution)/shard_map/ppermute | solution.py:236
  9.5 0.7 collective-permute-done.1.refs_4_
  10.2 1.2 %collective-permute-done.refs_3_ = f32[4,4,4,512]{3,2,1,0:T(4,128)S(1)} collective-permute-done((f32[4,4,4,512]{3,2,1,0:T(4,128)S(1)}, f32[4,4,4,512]{3,2,1,0:T(4,128)S(1)}, u32[]{:S(2)}, u32[]{:S(2)}) %collective-permute-start) | collective-permute-done | bytes 131104 | tf_op jit(solution)/shard_map/ppermute | solution.py:236
  11.4 0.0 copy-done.1
  11.4 1.6 %slab.1 = (f32[4,4,4,8,128]{4,3,2,1,0:T(8,128)}, f32[4,4,4,32,128]{4,3,2,1,0:T(8,128)S(1)}) custom-call(s32[4,8]{1,0:T(4,128)} %bitcast.2, s32[2]{0:T(128)} %vids.3, f32[4,4,16,512]{3,2,1,0:T(8,128)S(1)} %copy-done.1, f32[4,4,4,512]{3,2,1,0:T(4,128)S(1)} %collective-permute-done.refs_3_, f32[4,4,4,512]{3,2,1,0:T(4,128)S(1)} %collective-permute-done.1.refs_4_), custom_call_target="tpu_custom_call" | custom-call | tf_op jit(solution)/shard_map/slab/pallas_call | solution.py:238
  13.0 5.4 %all-to-all-start = ((f32[4,4,4,8,128]{4,3,2,1,0:T(8,128)}), f32[4,4,4,8,128]{4,3,2,1,0:T(8,128)S(1)}, u32[]{:S(2)}, u32[]{:S(2)}) async-start(f32[4,4,4,8,128]{4,3,2,1,0:T(8,128)} %get-tuple-element.12), calls=%async_computation | async-start | bytes 524288 | tf_op jit(solution)/shard_map/all_to_all | solution.py:234
  18.4 7.6 %all-to-all-done.agg = f32[4,4,4,8,128]{4,3,2,1,0:T(8,128)S(1)} async-done(((f32[4,4,4,8,128]{4,3,2,1,0:T(8,128)}), f32[4,4,4,8,128]{4,3,2,1,0:T(8,128)S(1)}, u32[]{:S(2)}, u32[]{:S(2)}) %all-to-all-start) | async-done | bytes 262176 | tf_op jit(solution)/shard_map/all_to_all | solution.py:234
  26.1 0.0 copy-start
  26.1 29.8 %all_to_all.20.groups = f32[4,4,4,8,128]{4,3,2,1,0:T(8,128)S(1)} all-to-all(f32[4,4,4,8,128]{4,3,2,1,0:T(8,128)S(1)} %group.1), channel_id=1, replica_groups={{0,224,352,384},{32,192,320,416},{64,160,288,448},{96,128,256,480},{1,2..., dimensions={0} | all-to-all | bytes 524288 | tf_op jit(solution)/shard_map/all_to_all | solution.py:234
  55.9 0.0 copy-done
  55.9 0.8 scan.1
  56.7 8.6 %all_to_all.21.got = f32[4,2,4,8,128]{4,3,2,1,0:T(8,128)S(1)} all-to-all(f32[4,2,4,8,128]{4,3,2,1,0:T(8,128)S(1)} %get-tuple-element.13), channel_id=1, replica_groups={{0,32,64,96},{224,192,160,128},{352,320,288,256},{384,416,448,480},{1,3..., dimensions={0} | all-to-all | bytes 262144 | tf_op jit(solution)/shard_map/all_to_all | solution.py:234
  65.3 3.9 %all-to-all-start.3 = ((f32[4,4,4,8,128]{4,3,2,1,0:T(8,128)}), f32[4,4,4,8,128]{4,3,2,1,0:T(8,128)S(1)}, u32[]{:S(2)}, u32[]{:S(2)}) async-start(f32[4,4,4,8,128]{4,3,2,1,0:T(8,128)} %get-tuple-element.19), calls=%async_computation.3 | async-start | bytes 524288 | tf_op jit(solution)/shard_map/all_to_all | solution.py:234
  69.1 0.9 %local.1 = (f32[2,4,4,16,128]{4,3,2,1,0:T(8,128)S(1)}, f32[2,4,4,16,128]{4,3,2,1,0:T(8,128)S(1)}) custom-call(s32[4,8]{1,0:T(4,128)} %bitcast.3, s32[2]{0:T(128)} %vids.3, f32[4,4,4,32,128]{4,3,2,1,0:T(8,128)S(1)} %get-tuple-element.14.refs_2_, f32[2,4,16,512]{3,2,1,0:T(8,128)S(1)} %copy-done), custom_call_target="tpu_custom_call" | custom-call | tf_op jit(solution)/shard_map/local/pallas_call | solution.py:257
  70.0 0.9 %edge.1 = (f32[4,4,4,512]{3,2,1,0:T(4,128)S(1)}, f32[4,4,4,512]{3,2,1,0:T(4,128)S(1)}) custom-call(s32[4,8]{1,0:T(4,128)} %bitcast.4, s32[2]{0:T(128)} %vids.3, f32[4,2,4,8,128]{4,3,2,1,0:T(8,128)S(1)} %all_to_all.21.got, f32[2,4,4,16,128]{4,3,2,1,0:T(8,128)S(1)} %get-tuple-element.15.absorb_part, f32[2,4,4,16,128]{4,3,2,1,0:T(8,128)S(1)} %get-tuple-element.16.emit_part, ...), custom_call_target="tpu_custom_call" | custom-call | tf_op jit(solution)/shard_map/edge/pallas_call | solution.py:277
  70.9 4.1 %collective-permute-start.2 = (f32[4,4,4,512]{3,2,1,0:T(4,128)S(1)}, f32[4,4,4,512]{3,2,1,0:T(4,128)S(1)}, u32[]{:S(2)}, u32[]{:S(2)}) collective-permute-start(f32[4,4,4,512]{3,2,1,0:T(4,128)S(1)} %get-tuple-element.17), channel_id=1, source_target_pairs={{0,1},{1,2},{2,3},{3,4},{4,5},{5,6},{6,7},{7,8},{8,9},{9,10},{10,1... | collective-permute-start | bytes 393224 | tf_op jit(solution)/shard_map/ppermute | solution.py:290
  75.0 2.1 %collective-permute-start.3 = (f32[4,4,4,512]{3,2,1,0:T(4,128)S(1)}, f32[4,4,4,512]{3,2,1,0:T(4,128)S(1)}, u32[]{:S(2)}, u32[]{:S(2)}) collective-permute-start(f32[4,4,4,512]{3,2,1,0:T(4,128)S(1)} %get-tuple-element.18), channel_id=1, source_target_pairs={{1,0},{2,1},{3,2},{4,3},{5,4},{6,5},{7,6},{8,7},{9,8},{10,9},{11,1... | collective-permute-start | bytes 393224 | tf_op jit(solution)/shard_map/ppermute | solution.py:291
  77.2 0.9 %main.1 = f32[4,4,16,512]{3,2,1,0:T(8,128)S(1)} custom-call(s32[4,8]{1,0:T(4,128)} %bitcast.5, s32[2]{0:T(128)} %vids.3, f32[4,2,4,8,128]{4,3,2,1,0:T(8,128)S(1)} %all_to_all.21.got, f32[2,4,4,16,128]{4,3,2,1,0:T(8,128)S(1)} %get-tuple-element.15.absorb_part, f32[2,4,4,16,128]{4,3,2,1,0:T(8,128)S(1)} %get-tuple-element.16.emit_part, ...), custom_call_target="tpu_custom_call" | custom-call | tf_op jit(solution)/shard_map/main/pallas_call | solution.py:292
  78.1 0.0 collective-permute-done.2.low
  78.1 5.3 %collective-permute-done.3.high = f32[4,4,4,512]{3,2,1,0:T(4,128)S(1)} collective-permute-done((f32[4,4,4,512]{3,2,1,0:T(4,128)S(1)}, f32[4,4,4,512]{3,2,1,0:T(4,128)S(1)}, u32[]{:S(2)}, u32[]{:S(2)}) %collective-permute-start.3) | collective-permute-done | bytes 131104 | tf_op jit(solution)/shard_map/ppermute | solution.py:291
  83.4 0.0 all-to-all-done.3.shown
  83.4 1.0 %join.1 = (f32[4,4,16,512]{3,2,1,0:T(8,128)}, f32[2,4,16,512]{3,2,1,0:T(8,128)}) custom-call(f32[4,4,16,512]{3,2,1,0:T(8,128)S(1)} %main.1, f32[4,4,4,512]{3,2,1,0:T(4,128)S(1)} %collective-permute-done.2.low, f32[4,4,4,512]{3,2,1,0:T(4,128)S(1)} %collective-permute-done.3.high, f32[4,4,4,8,128]{4,3,2,1,0:T(8,128)S(1)} %all-to-all-done.3.shown), custom_call_target="tpu_custom_call" | custom-call | tf_op jit(solution)/shard_map/join/pallas_call | solution.py:302
  (1 shorter events, 0.0 us)
Async XLA Ops:
  0.6 10.8 %copy-start.1 = (f32[4,4,16,512]{3,2,1,0:T(8,128)S(1)}, f32[4,4,16,512]{3,2,1,0:T(8,128)}, u32[]{:S(2)}) copy-start(f32[4,4,16,512]{3,2,1,0:T(8,128)} %refs_2_.1) | copy-start | bytes 1572868
  1.8 8.4 %collective-permute-start.1 = (f32[4,4,4,512]{3,2,1,0:T(4,128)S(1)}, f32[4,4,4,512]{3,2,1,0:T(4,128)S(1)}, u32[]{:S(2)}, u32[]{:S(2)}) collective-permute-start(f32[4,4,4,512]{3,2,1,0:T(4,128)S(1)} %get-tuple-element.22), channel_id=1, source_target_pairs={{1,0},{2,1},{3,2},{4,3},{5,4},{6,5},{7,6},{8,7},{9,8},{10,9},{11,1... | collective-permute-start | bytes 393224 | tf_op jit(solution)/shard_map/ppermute | solution.py:237
  4.4 7.0 %collective-permute-start = (f32[4,4,4,512]{3,2,1,0:T(4,128)S(1)}, f32[4,4,4,512]{3,2,1,0:T(4,128)S(1)}, u32[]{:S(2)}, u32[]{:S(2)}) collective-permute-start(f32[4,4,4,512]{3,2,1,0:T(4,128)S(1)} %get-tuple-element.23), channel_id=1, source_target_pairs={{0,1},{1,2},{2,3},{3,4},{4,5},{5,6},{6,7},{7,8},{8,9},{9,10},{10,1... | collective-permute-start | bytes 393224 | tf_op jit(solution)/shard_map/ppermute | solution.py:236
  13.0 13.1 %all-to-all-start = ((f32[4,4,4,8,128]{4,3,2,1,0:T(8,128)}), f32[4,4,4,8,128]{4,3,2,1,0:T(8,128)S(1)}, u32[]{:S(2)}, u32[]{:S(2)}) async-start(f32[4,4,4,8,128]{4,3,2,1,0:T(8,128)} %get-tuple-element.12), calls=%async_computation | async-start | bytes 524288 | tf_op jit(solution)/shard_map/all_to_all | solution.py:234
  26.1 29.8 %copy-start = (f32[2,4,16,512]{3,2,1,0:T(8,128)S(1)}, f32[2,4,16,512]{3,2,1,0:T(8,128)}, u32[]{:S(2)}) copy-start(f32[2,4,16,512]{3,2,1,0:T(8,128)} %w.5) | copy-start | bytes 786436
  65.3 18.2 %all-to-all-start.3 = ((f32[4,4,4,8,128]{4,3,2,1,0:T(8,128)}), f32[4,4,4,8,128]{4,3,2,1,0:T(8,128)S(1)}, u32[]{:S(2)}, u32[]{:S(2)}) async-start(f32[4,4,4,8,128]{4,3,2,1,0:T(8,128)} %get-tuple-element.19), calls=%async_computation.3 | async-start | bytes 524288 | tf_op jit(solution)/shard_map/all_to_all | solution.py:234
  70.9 7.2 %collective-permute-start.2 = (f32[4,4,4,512]{3,2,1,0:T(4,128)S(1)}, f32[4,4,4,512]{3,2,1,0:T(4,128)S(1)}, u32[]{:S(2)}, u32[]{:S(2)}) collective-permute-start(f32[4,4,4,512]{3,2,1,0:T(4,128)S(1)} %get-tuple-element.17), channel_id=1, source_target_pairs={{0,1},{1,2},{2,3},{3,4},{4,5},{5,6},{6,7},{7,8},{8,9},{9,10},{10,1... | collective-permute-start | bytes 393224 | tf_op jit(solution)/shard_map/ppermute | solution.py:290
  75.0 8.4 %collective-permute-start.3 = (f32[4,4,4,512]{3,2,1,0:T(4,128)S(1)}, f32[4,4,4,512]{3,2,1,0:T(4,128)S(1)}, u32[]{:S(2)}, u32[]{:S(2)}) collective-permute-start(f32[4,4,4,512]{3,2,1,0:T(4,128)S(1)} %get-tuple-element.18), channel_id=1, source_target_pairs={{1,0},{2,1},{3,2},{4,3},{5,4},{6,5},{7,6},{8,7},{9,8},{10,9},{11,1... | collective-permute-start | bytes 393224 | tf_op jit(solution)/shard_map/ppermute | solution.py:291

commit v5 on v4

--- a/solution.py
+++ b/solution.py
@@ -5,24 +5,36 @@
 from jax.experimental.pallas import tpu as pltpu
 from jax.sharding import PartitionSpec as P
 
+
 HALO = 4
 LANES = 128
 VMEM = pl.BlockSpec(memory_space=pltpu.VMEM)
 SMEM = pl.BlockSpec(memory_space=pltpu.SMEM)
-
-
-def slab_kernel(depth_total, offs, vids, vol, low, high, agg, ext):
+LIMIT = pltpu.CompilerParams(vmem_limit_bytes=16 * 1024 * 1024)
+
+
+def fill_kernel(vol, ext):
     channels, slabs, rows, cols = vol.shape
+    for c in range(channels):
+        for k in range(slabs):
+            for t in range(cols // LANES):
+                ext[c, k, t, 8 : 8 + rows, :] = vol[c, k, :, pl.ds(t * LANES, LANES)]
+
+
+def slab_kernel(depth_total, offs, vids, strip, inner, outer, own, agg, ext):
+    del own
+    channels, slabs, tiles, rows = ext.shape[:4]
+    rows -= 16
     views = vids.shape[0]
-    tiles = cols // LANES
     bands = rows // 8
+    odd = lax.rem(strip[0], 2) == 1
     for c in range(channels):
         for k in range(slabs):
             for t in range(tiles):
                 lanes = pl.ds(t * LANES, LANES)
-                ext[c, k, t, 4:8, :] = low[c, k, :, lanes]
-                ext[c, k, t, 8 : 8 + rows, :] = vol[c, k, :, lanes]
-                ext[c, k, t, 8 + rows : 12 + rows, :] = high[c, k, :, lanes]
+                near, far = inner[c, k, :, lanes], outer[c, k, :, lanes]
+                ext[c, k, t, 4:8, :] = jnp.where(odd, near, far)
+                ext[c, k, t, 8 + rows : 12 + rows, :] = jnp.where(odd, far, near)
     for v in range(views):
         starts = [8 - offs[k, vids[v]] for k in range(slabs)]
         for t in range(tiles):
@@ -126,7 +138,7 @@
             enter = passed + sum(weight[c] * agg[order[j], 1 + c, t] for c in range(3))
 
 
-def pixel_grads(got, absorb_part, emit_part, w, v, t, tiles, bands, slabs):
+def pixel_grads(got, absorb_part, emit_part, w, v, t, bands, slabs):
     lanes = pl.ds(t * LANES, LANES)
     owners = [v * bands + b for b in range(bands)]
     front = jnp.concatenate([got[n, 0, t] for n in owners], axis=0)
@@ -139,17 +151,18 @@
         yield k, parts
 
 
-def edge_kernel(offs, vids, got, absorb_part, emit_part, w, low, high, shifted):
+def edge_kernel(offs, vids, strip, got, absorb_part, emit_part, w, inner, outer, shifted):
     views, channels, rows, cols = w.shape
-    slabs = low.shape[1]
+    slabs = inner.shape[1]
     tiles = cols // LANES
     bands = rows // 8
+    odd = lax.rem(strip[0], 2) == 1
     edge = jnp.zeros((8, LANES), jnp.float32)
     moves = [[offs[k, vids[v]] for k in range(slabs)] for v in range(views)]
     for t in range(tiles):
         lanes = pl.ds(t * LANES, LANES)
         for v in range(views):
-            grads = pixel_grads(got, absorb_part, emit_part, w, v, t, tiles, bands, slabs)
+            grads = pixel_grads(got, absorb_part, emit_part, w, v, t, bands, slabs)
             for k, parts in grads:
                 for c in range(channels):
                     shifted[v, k, c, t, 0:8, :] = edge
@@ -164,8 +177,9 @@
                         for v in range(views)
                     )
 
-                low[c, k, :, lanes] = total(4)
-                high[c, k, :, lanes] = total(8 + rows)
+                low, high = total(4), total(8 + rows)
+                inner[c, k, :, lanes] = jnp.where(odd, low, high)
+                outer[c, k, :, lanes] = jnp.where(odd, high, low)
 
 
 def main_kernel(offs, vids, got, absorb_part, emit_part, w, main, shifted):
@@ -178,7 +192,7 @@
     for t in range(tiles):
         lanes = pl.ds(t * LANES, LANES)
         for v in range(views):
-            grads = pixel_grads(got, absorb_part, emit_part, w, v, t, tiles, bands, slabs)
+            grads = pixel_grads(got, absorb_part, emit_part, w, v, t, bands, slabs)
             for k, parts in grads:
                 for c in range(channels):
                     shifted[v, k, c, t, 4:8, :] = edge
@@ -191,13 +205,15 @@
                 )
 
 
-def join_kernel(main, low, high, shown, out, image):
+def join_kernel(strip, main, inner, outer, shown, out, image):
     rows = main.shape[2]
     views, channels, _, cols = image.shape
     bands = rows // 8
-    out[:, :, 0:4, :] = main[:, :, 0:4, :] + low[...]
+    odd = lax.rem(strip[0], 2) == 1
+    near, far = inner[...], outer[...]
+    out[:, :, 0:4, :] = main[:, :, 0:4, :] + jnp.where(odd, near, far)
     out[:, :, 4 : rows - 4, :] = main[:, :, 4 : rows - 4, :]
-    out[:, :, rows - 4 :, :] = main[:, :, rows - 4 :, :] + high[...]
+    out[:, :, rows - 4 :, :] = main[:, :, rows - 4 :, :] + jnp.where(odd, far, near)
     for v in range(views):
         for b in range(bands):
             for t in range(cols // LANES):
@@ -222,8 +238,8 @@
     near = [[size * g + i for i in range(size)] for g in range(count // size)]
     near = [row[::-1] if g in (1, 2) else row for g, row in enumerate(near)]
     far = [[row[i] for row in near] for i in range(size)]
-    up = [(i, i + 1) for i in range(strips - 1)]
-    down = [(i + 1, i) for i in range(strips - 1)]
+    pairs = [(i, i ^ 1) for i in range(strips)]
+    links = [(i, ((i + 1) ^ 1) - 1) for i in range(1, strips - 1)]
     f32 = lambda *shape: jax.ShapeDtypeStruct(shape, jnp.float32)
     kept = lambda *shape: pltpu.VMEM(shape, jnp.float32)
     table = offsets.T
@@ -233,27 +249,32 @@
     def swap(x, groups):
         return lax.all_to_all(x, "depth", 0, 0, tiled=True, axis_index_groups=groups)
 
-    low = lax.ppermute(volume[:, :, rows - HALO :], "lat", up)
-    high = lax.ppermute(volume[:, :, :HALO], "lat", down)
+    strip = lax.axis_index("lat").reshape(1).astype(jnp.int32)
+    odd = (strip & 1) == 1
+    first, last = volume[:, :, :HALO], volume[:, :, rows - HALO :]
+    outer = lax.ppermute(jnp.where(odd, last, first), "lat", links)
+    inner = lax.ppermute(jnp.where(odd, first, last), "lat", pairs)
+    own = pl.pallas_call(
+        fill_kernel,
+        out_shape=kept(channels, slabs, tiles, rows + 16, LANES),
+        in_specs=[VMEM],
+        out_specs=VMEM,
+        compiler_params=LIMIT,
+        name="fill",
+    )(on_chip(volume))
     agg, ext = pl.pallas_call(
         lambda *refs: slab_kernel(depth_total, *refs),
         out_shape=(
             kept(size, 4, tiles, 8, LANES),
             kept(channels, slabs, tiles, rows + 16, LANES),
         ),
-        in_specs=[SMEM, SMEM, VMEM, VMEM, VMEM],
-        out_specs=(VMEM, VMEM),
+        in_specs=[SMEM, SMEM, SMEM, VMEM, VMEM, VMEM],
+        out_specs=(VMEM, VMEM),
+        input_output_aliases={5: 1},
+        compiler_params=LIMIT,
         name="slab",
-    )(table, view_ids, on_chip(volume), on_chip(low), on_chip(high))
-    agg = on_chip(swap(agg, near))
-    grouped = pl.pallas_call(
-        group_kernel,
-        out_shape=kept(count // size, 4, tiles, 8, LANES),
-        in_specs=[SMEM, VMEM],
-        out_specs=VMEM,
-        name="group",
-    )(place, agg)
-    groups = on_chip(swap(grouped, far))
+    )(table, view_ids, strip, on_chip(inner), on_chip(outer), on_chip(own))
+    agg = swap(agg, near)
     absorb_part, emit_part = pl.pallas_call(
         lambda *refs: local_kernel(depth_total, *refs),
         out_shape=(
@@ -262,33 +283,47 @@
         ),
         in_specs=[SMEM, SMEM, VMEM, VMEM],
         out_specs=(VMEM, VMEM),
+        compiler_params=LIMIT,
         name="local",
     )(table, view_ids, on_chip(ext), w)
+    agg, absorb_part = lax.optimization_barrier((agg, absorb_part))
+    agg = on_chip(agg)
+    grouped = pl.pallas_call(
+        group_kernel,
+        out_shape=kept(count // size, 4, tiles, 8, LANES),
+        in_specs=[SMEM, VMEM],
+        out_specs=VMEM,
+        compiler_params=LIMIT,
+        name="group",
+    )(place, agg)
+    groups = on_chip(swap(grouped, far))
     sent, shown = pl.pallas_call(
         scan_kernel,
         out_shape=(kept(size, 2, tiles, 8, LANES), kept(size, 4, tiles, 8, LANES)),
         in_specs=[SMEM, VMEM, VMEM, VMEM],
         out_specs=(VMEM, VMEM),
+        compiler_params=LIMIT,
         name="scan",
     )(place, agg, groups, w)
     got = on_chip(swap(sent, near))
     shown = swap(shown, near)
 
-    to_low, to_high = pl.pallas_call(
+    to_inner, to_outer = pl.pallas_call(
         edge_kernel,
         out_shape=(
             kept(channels, slabs, HALO, cols),
             kept(channels, slabs, HALO, cols),
         ),
-        in_specs=[SMEM, SMEM, VMEM, VMEM, VMEM, VMEM],
+        in_specs=[SMEM, SMEM, SMEM, VMEM, VMEM, VMEM, VMEM],
         out_specs=(VMEM, VMEM),
         scratch_shapes=[
             pltpu.VMEM((views, slabs, channels, tiles, rows + 16, LANES), jnp.float32)
         ],
+        compiler_params=LIMIT,
         name="edge",
-    )(table, view_ids, got, on_chip(absorb_part), on_chip(emit_part), w)
-    from_low = lax.ppermute(to_high, "lat", up)
-    from_high = lax.ppermute(to_low, "lat", down)
+    )(table, view_ids, strip, got, on_chip(absorb_part), on_chip(emit_part), w)
+    from_outer = lax.ppermute(to_outer, "lat", links)
+    from_inner = lax.ppermute(to_inner, "lat", pairs)
     main = pl.pallas_call(
         main_kernel,
         out_shape=kept(channels, slabs, rows, cols),
@@ -297,15 +332,17 @@
         scratch_shapes=[
             pltpu.VMEM((views, slabs, channels, tiles, rows + 16, LANES), jnp.float32)
         ],
+        compiler_params=LIMIT,
         name="main",
     )(table, view_ids, got, on_chip(absorb_part), on_chip(emit_part), w)
     grad_out, image_out = pl.pallas_call(
         join_kernel,
         out_shape=(f32(channels, slabs, rows, cols), f32(views, channels, rows, cols)),
-        in_specs=[VMEM, VMEM, VMEM, VMEM],
-        out_specs=(VMEM, VMEM),
+        in_specs=[SMEM, VMEM, VMEM, VMEM, VMEM],
+        out_specs=(VMEM, VMEM),
+        compiler_params=LIMIT,
         name="join",
-    )(on_chip(main), on_chip(from_low), on_chip(from_high), on_chip(shown))
+    )(strip, on_chip(main), on_chip(from_inner), on_chip(from_outer), on_chip(shown))
     return (image_out, grad_out)
 
 

time: 85 us -> 81 us (0.953)
  the two profiles are of different devices: /device:TPU:59 before, /device:TPU:61 now
where the time goes in v5:
time: 81 us; the launch traced here: 80.6 us
  blocking collectives  36.9 us (46%)
  starting transfers between devices  21.8 us (27%)
  waiting for transfers between devices  14.4 us (18%)
  Pallas kernels  5.59 us (7%)
  other arithmetic  1.14 us (1%)
    all_to_all x2, blocking collectives, swap(): lax.all_to_all(x, 'depth', 0, 0, tiled=True, axis_index_groups=groups)  36.9 us
    all_to_all x2, starting transfers between devices, swap(): lax.all_to_all(x, 'depth', 0, 0, tiled=True, axis_index_groups=groups)  9.44 us
    all_to_all x2, waiting for transfers between devices, swap(): lax.all_to_all(x, 'depth', 0, 0, tiled=True, axis_index_groups=groups)  6.02 us
    ppermute x1, waiting for transfers between devices, on_device(): from_outer = lax.ppermute(to_outer, 'lat', links)  5.07 us
    ppermute x1, starting transfers between devices, on_device(): from_inner = lax.ppermute(to_inner, 'lat', pairs)  4.87 us
    ppermute x1, waiting for transfers between devices, on_device(): outer = lax.ppermute(jnp.where(odd, last, first), 'lat', links)  3.34 us
    ppermute x1, starting transfers between devices, on_device(): outer = lax.ppermute(jnp.where(odd, last, first), 'lat', links)  3.04 us
    ppermute x1, starting transfers between devices, on_device(): from_outer = lax.ppermute(to_outer, 'lat', links)  2.49 us
  transfers between devices with their start and end apart: 6, of which 3 were waited for; matrix products, arithmetic and copies ran while one was open for 0% of the time, Pallas kernels for 3%

profile of v5, /device:TPU:61, one launch (start us, length us, event | category | flops | bytes accessed | tf_op | source)
XLA Modules:
  0.0 80.6 jit_solution(11610627287823986947)
XLA Ops:
  0.6 0.0 copy-start.1
  0.6 1.1 %slice_select_fusion = (f32[4,4,4,512]{3,2,1,0:T(4,128)S(1)}, f32[4,4,4,512]{3,2,1,0:T(4,128)S(1)}) fusion(f32[4,4,16,512]{3,2,1,0:T(8,128)} %vol.1, pred[]{:T(512)} %bitcast.3), kind=kLoop, calls=%fused_computation | loop fusion | flops 65536 | bytes 524289 | tf_op jit(solution)/shard_map/jit(_where)/select_n | solution.py:255
  1.8 3.0 %collective-permute-start.1 = (f32[4,4,4,512]{3,2,1,0:T(4,128)S(1)}, f32[4,4,4,512]{3,2,1,0:T(4,128)S(1)}, u32[]{:S(2)}, u32[]{:S(2)}) collective-permute-start(f32[4,4,4,512]{3,2,1,0:T(4,128)S(1)} %get-tuple-element.26), channel_id=1, source_target_pairs={{1,2},{2,1},{3,4},{4,3},{5,6},{6,5},{7,8},{8,7},{9,10},{10,9},{11,... | collective-permute-start | bytes 393224 | tf_op jit(solution)/shard_map/ppermute | solution.py:255
  4.8 1.9 %collective-permute-start = (f32[4,4,4,512]{3,2,1,0:T(4,128)S(1)}, f32[4,4,4,512]{3,2,1,0:T(4,128)S(1)}, u32[]{:S(2)}, u32[]{:S(2)}) collective-permute-start(f32[4,4,4,512]{3,2,1,0:T(4,128)S(1)} %get-tuple-element.27), channel_id=1, source_target_pairs={{0,1},{1,0},{2,3},{3,2},{4,5},{5,4},{6,7},{7,6},{8,9},{9,8},{10,11... | collective-permute-start | bytes 393224 | tf_op jit(solution)/shard_map/ppermute | solution.py:256
  6.8 0.0 copy-done.1
  6.8 0.0 copy-start.2
  6.8 0.0 copy-start.3
  6.8 3.3 %collective-permute-done.1.refs_4_ = f32[4,4,4,512]{3,2,1,0:T(4,128)S(1)} collective-permute-done((f32[4,4,4,512]{3,2,1,0:T(4,128)S(1)}, f32[4,4,4,512]{3,2,1,0:T(4,128)S(1)}, u32[]{:S(2)}, u32[]{:S(2)}) %collective-permute-start.1) | collective-permute-done | bytes 131104 | tf_op jit(solution)/shard_map/ppermute | solution.py:255
  10.2 0.0 collective-permute-done.refs_3_
  10.2 0.0 copy-done.2
  10.2 0.0 copy-done.3
  10.2 1.4 %slab.1 = (f32[4,4,4,8,128]{4,3,2,1,0:T(8,128)}, f32[4,4,4,32,128]{4,3,2,1,0:T(8,128)S(1)}) custom-call(s32[4,8]{1,0:T(4,128)S(1)} %bitcast.4, s32[2]{0:T(128)S(1)} %copy-done.3, s32[1]{0:T(128)} %bitcast.refs_2_.strip, f32[4,4,4,512]{3,2,1,0:T(4,128)S(1)} %collective-permute-done.refs_3_, ...), custom_call_target="tpu_custom_call", output_to_operand_aliasing={{1}: (5, {})} | custom-call | tf_op jit(solution)/shard_map/slab/pallas_call | solution.py:265
  11.6 0.0 copy-start
  11.6 5.6 %all-to-all-start = ((f32[4,4,4,8,128]{4,3,2,1,0:T(8,128)}), f32[4,4,4,8,128]{4,3,2,1,0:T(8,128)S(1)}, u32[]{:S(2)}, u32[]{:S(2)}) async-start(f32[4,4,4,8,128]{4,3,2,1,0:T(8,128)} %get-tuple-element.14), calls=%async_computation | async-start | bytes 524288 | tf_op jit(solution)/shard_map/all_to_all | solution.py:250
  17.2 0.0 copy-done
  17.2 0.7 local.1
  17.9 6.0 %all-to-all-done.agg = f32[4,4,4,8,128]{4,3,2,1,0:T(8,128)S(1)} async-done(((f32[4,4,4,8,128]{4,3,2,1,0:T(8,128)}), f32[4,4,4,8,128]{4,3,2,1,0:T(8,128)S(1)}, u32[]{:S(2)}, u32[]{:S(2)}) %all-to-all-start) | async-done | bytes 262176 | tf_op jit(solution)/shard_map/all_to_all | solution.py:250
  24.0 29.6 %all_to_all.20.groups = f32[4,4,4,8,128]{4,3,2,1,0:T(8,128)S(1)} all-to-all(f32[4,4,4,8,128]{4,3,2,1,0:T(8,128)S(1)} %group.1), channel_id=1, replica_groups={{0,224,352,384},{32,192,320,416},{64,160,288,448},{96,128,256,480},{1,2..., dimensions={0} | all-to-all | bytes 524288 | tf_op jit(solution)/shard_map/all_to_all | solution.py:250
  53.6 0.8 scan.1
  54.4 7.3 %all_to_all.21.got = f32[4,2,4,8,128]{4,3,2,1,0:T(8,128)S(1)} all-to-all(f32[4,2,4,8,128]{4,3,2,1,0:T(8,128)S(1)} %get-tuple-element.18), channel_id=1, replica_groups={{0,32,64,96},{224,192,160,128},{352,320,288,256},{384,416,448,480},{1,3..., dimensions={0} | all-to-all | bytes 262144 | tf_op jit(solution)/shard_map/all_to_all | solution.py:250
  61.7 3.9 %all-to-all-start.3 = ((f32[4,4,4,8,128]{4,3,2,1,0:T(8,128)}), f32[4,4,4,8,128]{4,3,2,1,0:T(8,128)S(1)}, u32[]{:S(2)}, u32[]{:S(2)}) async-start(f32[4,4,4,8,128]{4,3,2,1,0:T(8,128)} %get-tuple-element.23), calls=%async_computation.3 | async-start | bytes 524288 | tf_op jit(solution)/shard_map/all_to_all | solution.py:250
  65.5 0.8 edge.1
  66.3 4.9 %collective-permute-start.2 = (f32[4,4,4,512]{3,2,1,0:T(4,128)S(1)}, f32[4,4,4,512]{3,2,1,0:T(4,128)S(1)}, u32[]{:S(2)}, u32[]{:S(2)}) collective-permute-start(f32[4,4,4,512]{3,2,1,0:T(4,128)S(1)} %get-tuple-element.21), channel_id=1, source_target_pairs={{0,1},{1,0},{2,3},{3,2},{4,5},{5,4},{6,7},{7,6},{8,9},{9,8},{10,11... | collective-permute-start | bytes 393224 | tf_op jit(solution)/shard_map/ppermute | solution.py:326
  71.2 2.5 %collective-permute-start.3 = (f32[4,4,4,512]{3,2,1,0:T(4,128)S(1)}, f32[4,4,4,512]{3,2,1,0:T(4,128)S(1)}, u32[]{:S(2)}, u32[]{:S(2)}) collective-permute-start(f32[4,4,4,512]{3,2,1,0:T(4,128)S(1)} %get-tuple-element.22), channel_id=1, source_target_pairs={{1,2},{2,1},{3,4},{4,3},{5,6},{6,5},{7,8},{8,7},{9,10},{10,9},{11,... | collective-permute-start | bytes 393224 | tf_op jit(solution)/shard_map/ppermute | solution.py:325
  73.7 0.8 %main.1 = f32[4,4,16,512]{3,2,1,0:T(8,128)S(1)} custom-call(s32[4,8]{1,0:T(4,128)S(1)} %bitcast.7, s32[2]{0:T(128)S(1)} %copy-done.3, f32[4,2,4,8,128]{4,3,2,1,0:T(8,128)S(1)} %all_to_all.21.got, f32[2,4,4,16,128]{4,3,2,1,0:T(8,128)S(1)} %get-tuple-element.19.absorb_part, f32[2,4,4,16,128]{4,3,2,1,0:T(8,128)S(1)} %get-tuple-element.20.emit_part, ...), custom_call_target="tpu_custom_call" | custom-call | tf_op jit(solution)/shard_map/main/pallas_call | solution.py:327
  74.5 0.0 collective-permute-done.2.inner
  74.5 5.1 %collective-permute-done.3.outer = f32[4,4,4,512]{3,2,1,0:T(4,128)S(1)} collective-permute-done((f32[4,4,4,512]{3,2,1,0:T(4,128)S(1)}, f32[4,4,4,512]{3,2,1,0:T(4,128)S(1)}, u32[]{:S(2)}, u32[]{:S(2)}) %collective-permute-start.3) | collective-permute-done | bytes 131104 | tf_op jit(solution)/shard_map/ppermute | solution.py:325
  79.6 0.0 all-to-all-done.3.shown
  79.6 1.0 %join.1 = (f32[4,4,16,512]{3,2,1,0:T(8,128)}, f32[2,4,16,512]{3,2,1,0:T(8,128)}) custom-call(s32[1]{0:T(128)} %bitcast.refs_2_.strip, f32[4,4,16,512]{3,2,1,0:T(8,128)S(1)} %main.1, f32[4,4,4,512]{3,2,1,0:T(4,128)S(1)} %collective-permute-done.2.inner, f32[4,4,4,512]{3,2,1,0:T(4,128)S(1)} %collective-permute-done.3.outer, ...), custom_call_target="tpu_custom_call" | custom-call | tf_op jit(solution)/shard_map/join/pallas_call | solution.py:338
  (2 shorter events, 0.1 us)
Async XLA Ops:
  0.6 6.1 %copy-start.1 = (f32[4,4,16,512]{3,2,1,0:T(8,128)S(1)}, f32[4,4,16,512]{3,2,1,0:T(8,128)}, u32[]{:S(2)}) copy-start(f32[4,4,16,512]{3,2,1,0:T(8,128)} %vol.1) | copy-start | bytes 1572868
  1.8 8.4 %collective-permute-start.1 = (f32[4,4,4,512]{3,2,1,0:T(4,128)S(1)}, f32[4,4,4,512]{3,2,1,0:T(4,128)S(1)}, u32[]{:S(2)}, u32[]{:S(2)}) collective-permute-start(f32[4,4,4,512]{3,2,1,0:T(4,128)S(1)} %get-tuple-element.26), channel_id=1, source_target_pairs={{1,2},{2,1},{3,4},{4,3},{5,6},{6,5},{7,8},{8,7},{9,10},{10,9},{11,... | collective-permute-start | bytes 393224 | tf_op jit(solution)/shard_map/ppermute | solution.py:255
  4.8 5.3 %collective-permute-start = (f32[4,4,4,512]{3,2,1,0:T(4,128)S(1)}, f32[4,4,4,512]{3,2,1,0:T(4,128)S(1)}, u32[]{:S(2)}, u32[]{:S(2)}) collective-permute-start(f32[4,4,4,512]{3,2,1,0:T(4,128)S(1)} %get-tuple-element.27), channel_id=1, source_target_pairs={{0,1},{1,0},{2,3},{3,2},{4,5},{5,4},{6,7},{7,6},{8,9},{9,8},{10,11... | collective-permute-start | bytes 393224 | tf_op jit(solution)/shard_map/ppermute | solution.py:256
  6.8 3.4 %copy-start.2 = (s32[8,4]{0,1:T(4,128)S(1)}, s32[8,4]{0,1:T(4,128)}, u32[]{:S(2)}) copy-start(s32[8,4]{0,1:T(4,128)} %param.5) | copy-start | bytes 388
  6.8 3.4 %copy-start.3 = (s32[2]{0:T(128)S(1)}, s32[2]{0:T(128)}, u32[]{:S(2)}) copy-start(s32[2]{0:T(128)} %vids.3) | copy-start | bytes 28
  11.6 5.6 %copy-start = (f32[2,4,16,512]{3,2,1,0:T(8,128)S(1)}, f32[2,4,16,512]{3,2,1,0:T(8,128)}, u32[]{:S(2)}) copy-start(f32[2,4,16,512]{3,2,1,0:T(8,128)} %w.5) | copy-start | bytes 786436
  11.6 12.3 %all-to-all-start = ((f32[4,4,4,8,128]{4,3,2,1,0:T(8,128)}), f32[4,4,4,8,128]{4,3,2,1,0:T(8,128)S(1)}, u32[]{:S(2)}, u32[]{:S(2)}) async-start(f32[4,4,4,8,128]{4,3,2,1,0:T(8,128)} %get-tuple-element.14), calls=%async_computation | async-start | bytes 524288 | tf_op jit(solution)/shard_map/all_to_all | solution.py:250
  61.7 17.9 %all-to-all-start.3 = ((f32[4,4,4,8,128]{4,3,2,1,0:T(8,128)}), f32[4,4,4,8,128]{4,3,2,1,0:T(8,128)S(1)}, u32[]{:S(2)}, u32[]{:S(2)}) async-start(f32[4,4,4,8,128]{4,3,2,1,0:T(8,128)} %get-tuple-element.23), calls=%async_computation.3 | async-start | bytes 524288 | tf_op jit(solution)/shard_map/all_to_all | solution.py:250
  66.3 8.2 %collective-permute-start.2 = (f32[4,4,4,512]{3,2,1,0:T(4,128)S(1)}, f32[4,4,4,512]{3,2,1,0:T(4,128)S(1)}, u32[]{:S(2)}, u32[]{:S(2)}) collective-permute-start(f32[4,4,4,512]{3,2,1,0:T(4,128)S(1)} %get-tuple-element.21), channel_id=1, source_target_pairs={{0,1},{1,0},{2,3},{3,2},{4,5},{5,4},{6,7},{7,6},{8,9},{9,8},{10,11... | collective-permute-start | bytes 393224 | tf_op jit(solution)/shard_map/ppermute | solution.py:326
  71.2 8.4 %collective-permute-start.3 = (f32[4,4,4,512]{3,2,1,0:T(4,128)S(1)}, f32[4,4,4,512]{3,2,1,0:T(4,128)S(1)}, u32[]{:S(2)}, u32[]{:S(2)}) collective-permute-start(f32[4,4,4,512]{3,2,1,0:T(4,128)S(1)} %get-tuple-element.22), channel_id=1, source_target_pairs={{1,2},{2,1},{3,4},{4,3},{5,6},{6,5},{7,8},{8,7},{9,10},{10,9},{11,... | collective-permute-start | bytes 393224 | tf_op jit(solution)/shard_map/ppermute | solution.py:325

commit v6 on v5

--- a/solution.py
+++ b/solution.py
@@ -81,9 +81,10 @@
 
 def seat(place, members):
     mine, member = lax.div(place[0], members), lax.rem(place[0], members)
-    turned = (mine == 1) | (mine == 2)
-    order = [jnp.where(turned, members - 1 - j, j) for j in range(members)]
-    return mine, jnp.where(turned, members - 1 - member, member), order
+    turned = mine >= 2
+    half = members // 2
+    order = [jnp.where(turned, (j + half) % members, j) for j in range(members)]
+    return mine, jnp.where(turned, lax.rem(member + half, members), member), order
 
 
 def group_kernel(place, agg, out):
@@ -236,7 +237,7 @@
     depth_total = slabs * count
     size = views * bands
     near = [[size * g + i for i in range(size)] for g in range(count // size)]
-    near = [row[::-1] if g in (1, 2) else row for g, row in enumerate(near)]
+    near = [row[size // 2 :] + row[: size // 2] if g >= 2 else row for g, row in enumerate(near)]
     far = [[row[i] for row in near] for i in range(size)]
     pairs = [(i, i ^ 1) for i in range(strips)]
     links = [(i, ((i + 1) ^ 1) - 1) for i in range(1, strips - 1)]

time: 81 us -> 80.2 us (level)
  starting transfers between devices: 21.8 us -> 20.9 us
where the time goes in v6:
time: 80.2 us; the launch traced here: 79.8 us
  blocking collectives  36.7 us (46%)
  starting transfers between devices  20.9 us (26%)
  waiting for transfers between devices  14.7 us (18%)
  Pallas kernels  5.57 us (7%)
  other arithmetic  1.14 us (1%)
    all_to_all x2, blocking collectives, swap(): lax.all_to_all(x, 'depth', 0, 0, tiled=True, axis_index_groups=groups)  36.7 us
    all_to_all x2, starting transfers between devices, swap(): lax.all_to_all(x, 'depth', 0, 0, tiled=True, axis_index_groups=groups)  9.64 us
    all_to_all x2, waiting for transfers between devices, swap(): lax.all_to_all(x, 'depth', 0, 0, tiled=True, axis_index_groups=groups)  6.02 us
    ppermute x1, waiting for transfers between devices, on_device(): from_outer = lax.ppermute(to_outer, 'lat', links)  5.35 us
    ppermute x1, starting transfers between devices, on_device(): from_inner = lax.ppermute(to_inner, 'lat', pairs)  4.07 us
    ppermute x1, waiting for transfers between devices, on_device(): outer = lax.ppermute(jnp.where(odd, last, first), 'lat', links)  3.34 us
    ppermute x1, starting transfers between devices, on_device(): outer = lax.ppermute(jnp.where(odd, last, first), 'lat', links)  3.04 us
    ppermute x1, starting transfers between devices, on_device(): from_outer = lax.ppermute(to_outer, 'lat', links)  2.21 us
  transfers between devices with their start and end apart: 6, of which 3 were waited for; matrix products, arithmetic and copies ran while one was open for 0% of the time, Pallas kernels for 3%

profile of v6, /device:TPU:61, one launch (start us, length us, event | category | flops | bytes accessed | tf_op | source)
XLA Modules:
  0.0 79.8 jit_solution(15116998017941750941)
XLA Ops:
  0.6 0.0 copy-start.1
  0.6 1.1 %slice_select_fusion = (f32[4,4,4,512]{3,2,1,0:T(4,128)S(1)}, f32[4,4,4,512]{3,2,1,0:T(4,128)S(1)}) fusion(f32[4,4,16,512]{3,2,1,0:T(8,128)} %vol.1, pred[]{:T(512)} %bitcast.3), kind=kLoop, calls=%fused_computation | loop fusion | flops 65536 | bytes 524289 | tf_op jit(solution)/shard_map/jit(_where)/select_n | solution.py:256
  1.8 3.0 %collective-permute-start.1 = (f32[4,4,4,512]{3,2,1,0:T(4,128)S(1)}, f32[4,4,4,512]{3,2,1,0:T(4,128)S(1)}, u32[]{:S(2)}, u32[]{:S(2)}) collective-permute-start(f32[4,4,4,512]{3,2,1,0:T(4,128)S(1)} %get-tuple-element.26), channel_id=1, source_target_pairs={{1,2},{2,1},{3,4},{4,3},{5,6},{6,5},{7,8},{8,7},{9,10},{10,9},{11,... | collective-permute-start | bytes 393224 | tf_op jit(solution)/shard_map/ppermute | solution.py:256
  4.8 1.9 %collective-permute-start = (f32[4,4,4,512]{3,2,1,0:T(4,128)S(1)}, f32[4,4,4,512]{3,2,1,0:T(4,128)S(1)}, u32[]{:S(2)}, u32[]{:S(2)}) collective-permute-start(f32[4,4,4,512]{3,2,1,0:T(4,128)S(1)} %get-tuple-element.27), channel_id=1, source_target_pairs={{0,1},{1,0},{2,3},{3,2},{4,5},{5,4},{6,7},{7,6},{8,9},{9,8},{10,11... | collective-permute-start | bytes 393224 | tf_op jit(solution)/shard_map/ppermute | solution.py:257
  6.8 0.0 copy-done.1
  6.8 0.0 copy-start.2
  6.8 0.0 copy-start.3
  6.8 3.3 %collective-permute-done.1.refs_4_ = f32[4,4,4,512]{3,2,1,0:T(4,128)S(1)} collective-permute-done((f32[4,4,4,512]{3,2,1,0:T(4,128)S(1)}, f32[4,4,4,512]{3,2,1,0:T(4,128)S(1)}, u32[]{:S(2)}, u32[]{:S(2)}) %collective-permute-start.1) | collective-permute-done | bytes 131104 | tf_op jit(solution)/shard_map/ppermute | solution.py:256
  10.2 0.0 collective-permute-done.refs_3_
  10.2 0.0 copy-done.2
  10.2 0.0 copy-done.3
  10.2 1.4 %slab.1 = (f32[4,4,4,8,128]{4,3,2,1,0:T(8,128)}, f32[4,4,4,32,128]{4,3,2,1,0:T(8,128)S(1)}) custom-call(s32[4,8]{1,0:T(4,128)S(1)} %bitcast.4, s32[2]{0:T(128)S(1)} %copy-done.3, s32[1]{0:T(128)} %bitcast.refs_2_.strip, f32[4,4,4,512]{3,2,1,0:T(4,128)S(1)} %collective-permute-done.refs_3_, ...), custom_call_target="tpu_custom_call", output_to_operand_aliasing={{1}: (5, {})} | custom-call | tf_op jit(solution)/shard_map/slab/pallas_call | solution.py:266
  11.6 0.0 copy-start
  11.6 5.6 %all-to-all-start = ((f32[4,4,4,8,128]{4,3,2,1,0:T(8,128)}), f32[4,4,4,8,128]{4,3,2,1,0:T(8,128)S(1)}, u32[]{:S(2)}, u32[]{:S(2)}) async-start(f32[4,4,4,8,128]{4,3,2,1,0:T(8,128)} %get-tuple-element.14), calls=%async_computation | async-start | bytes 524288 | tf_op jit(solution)/shard_map/all_to_all | solution.py:251
  17.2 0.0 copy-done
  17.2 0.7 local.1
  17.9 6.0 %all-to-all-done.agg = f32[4,4,4,8,128]{4,3,2,1,0:T(8,128)S(1)} async-done(((f32[4,4,4,8,128]{4,3,2,1,0:T(8,128)}), f32[4,4,4,8,128]{4,3,2,1,0:T(8,128)S(1)}, u32[]{:S(2)}, u32[]{:S(2)}) %all-to-all-start) | async-done | bytes 262176 | tf_op jit(solution)/shard_map/all_to_all | solution.py:251
  24.0 29.9 %all_to_all.20.groups = f32[4,4,4,8,128]{4,3,2,1,0:T(8,128)S(1)} all-to-all(f32[4,4,4,8,128]{4,3,2,1,0:T(8,128)S(1)} %group.1), channel_id=1, replica_groups={{0,128,320,448},{32,160,352,480},{64,192,256,384},{96,224,288,416},{1,1..., dimensions={0} | all-to-all | bytes 524288 | tf_op jit(solution)/shard_map/all_to_all | solution.py:251
  53.9 0.8 scan.1
  54.6 6.8 %all_to_all.21.got = f32[4,2,4,8,128]{4,3,2,1,0:T(8,128)S(1)} all-to-all(f32[4,2,4,8,128]{4,3,2,1,0:T(8,128)S(1)} %get-tuple-element.18), channel_id=1, replica_groups={{0,32,64,96},{128,160,192,224},{320,352,256,288},{448,480,384,416},{1,3..., dimensions={0} | all-to-all | bytes 262144 | tf_op jit(solution)/shard_map/all_to_all | solution.py:251
  61.4 4.1 %all-to-all-start.3 = ((f32[4,4,4,8,128]{4,3,2,1,0:T(8,128)}), f32[4,4,4,8,128]{4,3,2,1,0:T(8,128)S(1)}, u32[]{:S(2)}, u32[]{:S(2)}) async-start(f32[4,4,4,8,128]{4,3,2,1,0:T(8,128)} %get-tuple-element.23), calls=%async_computation.3 | async-start | bytes 524288 | tf_op jit(solution)/shard_map/all_to_all | solution.py:251
  65.5 0.8 edge.1
  66.3 4.1 %collective-permute-start.2 = (f32[4,4,4,512]{3,2,1,0:T(4,128)S(1)}, f32[4,4,4,512]{3,2,1,0:T(4,128)S(1)}, u32[]{:S(2)}, u32[]{:S(2)}) collective-permute-start(f32[4,4,4,512]{3,2,1,0:T(4,128)S(1)} %get-tuple-element.21), channel_id=1, source_target_pairs={{0,1},{1,0},{2,3},{3,2},{4,5},{5,4},{6,7},{7,6},{8,9},{9,8},{10,11... | collective-permute-start | bytes 393224 | tf_op jit(solution)/shard_map/ppermute | solution.py:327
  70.4 2.2 %collective-permute-start.3 = (f32[4,4,4,512]{3,2,1,0:T(4,128)S(1)}, f32[4,4,4,512]{3,2,1,0:T(4,128)S(1)}, u32[]{:S(2)}, u32[]{:S(2)}) collective-permute-start(f32[4,4,4,512]{3,2,1,0:T(4,128)S(1)} %get-tuple-element.22), channel_id=1, source_target_pairs={{1,2},{2,1},{3,4},{4,3},{5,6},{6,5},{7,8},{8,7},{9,10},{10,9},{11,... | collective-permute-start | bytes 393224 | tf_op jit(solution)/shard_map/ppermute | solution.py:326
  72.6 0.8 %main.1 = f32[4,4,16,512]{3,2,1,0:T(8,128)S(1)} custom-call(s32[4,8]{1,0:T(4,128)S(1)} %bitcast.7, s32[2]{0:T(128)S(1)} %copy-done.3, f32[4,2,4,8,128]{4,3,2,1,0:T(8,128)S(1)} %all_to_all.21.got, f32[2,4,4,16,128]{4,3,2,1,0:T(8,128)S(1)} %get-tuple-element.19.absorb_part, f32[2,4,4,16,128]{4,3,2,1,0:T(8,128)S(1)} %get-tuple-element.20.emit_part, ...), custom_call_target="tpu_custom_call" | custom-call | tf_op jit(solution)/shard_map/main/pallas_call | solution.py:328
  73.4 0.0 collective-permute-done.2.inner
  73.4 5.3 %collective-permute-done.3.outer = f32[4,4,4,512]{3,2,1,0:T(4,128)S(1)} collective-permute-done((f32[4,4,4,512]{3,2,1,0:T(4,128)S(1)}, f32[4,4,4,512]{3,2,1,0:T(4,128)S(1)}, u32[]{:S(2)}, u32[]{:S(2)}) %collective-permute-start.3) | collective-permute-done | bytes 131104 | tf_op jit(solution)/shard_map/ppermute | solution.py:326
  78.8 0.0 all-to-all-done.3.shown
  78.8 1.0 %join.1 = (f32[4,4,16,512]{3,2,1,0:T(8,128)}, f32[2,4,16,512]{3,2,1,0:T(8,128)}) custom-call(s32[1]{0:T(128)} %bitcast.refs_2_.strip, f32[4,4,16,512]{3,2,1,0:T(8,128)S(1)} %main.1, f32[4,4,4,512]{3,2,1,0:T(4,128)S(1)} %collective-permute-done.2.inner, f32[4,4,4,512]{3,2,1,0:T(4,128)S(1)} %collective-permute-done.3.outer, ...), custom_call_target="tpu_custom_call" | custom-call | tf_op jit(solution)/shard_map/join/pallas_call | solution.py:339
  (2 shorter events, 0.1 us)
Async XLA Ops:
  0.6 6.1 %copy-start.1 = (f32[4,4,16,512]{3,2,1,0:T(8,128)S(1)}, f32[4,4,16,512]{3,2,1,0:T(8,128)}, u32[]{:S(2)}) copy-start(f32[4,4,16,512]{3,2,1,0:T(8,128)} %vol.1) | copy-start | bytes 1572868
  1.8 8.4 %collective-permute-start.1 = (f32[4,4,4,512]{3,2,1,0:T(4,128)S(1)}, f32[4,4,4,512]{3,2,1,0:T(4,128)S(1)}, u32[]{:S(2)}, u32[]{:S(2)}) collective-permute-start(f32[4,4,4,512]{3,2,1,0:T(4,128)S(1)} %get-tuple-element.26), channel_id=1, source_target_pairs={{1,2},{2,1},{3,4},{4,3},{5,6},{6,5},{7,8},{8,7},{9,10},{10,9},{11,... | collective-permute-start | bytes 393224 | tf_op jit(solution)/shard_map/ppermute | solution.py:256
  4.8 5.3 %collective-permute-start = (f32[4,4,4,512]{3,2,1,0:T(4,128)S(1)}, f32[4,4,4,512]{3,2,1,0:T(4,128)S(1)}, u32[]{:S(2)}, u32[]{:S(2)}) collective-permute-start(f32[4,4,4,512]{3,2,1,0:T(4,128)S(1)} %get-tuple-element.27), channel_id=1, source_target_pairs={{0,1},{1,0},{2,3},{3,2},{4,5},{5,4},{6,7},{7,6},{8,9},{9,8},{10,11... | collective-permute-start | bytes 393224 | tf_op jit(solution)/shard_map/ppermute | solution.py:257
  6.8 3.4 %copy-start.2 = (s32[8,4]{0,1:T(4,128)S(1)}, s32[8,4]{0,1:T(4,128)}, u32[]{:S(2)}) copy-start(s32[8,4]{0,1:T(4,128)} %param.5) | copy-start | bytes 388
  6.8 3.4 %copy-start.3 = (s32[2]{0:T(128)S(1)}, s32[2]{0:T(128)}, u32[]{:S(2)}) copy-start(s32[2]{0:T(128)} %vids.3) | copy-start | bytes 28
  11.6 5.6 %copy-start = (f32[2,4,16,512]{3,2,1,0:T(8,128)S(1)}, f32[2,4,16,512]{3,2,1,0:T(8,128)}, u32[]{:S(2)}) copy-start(f32[2,4,16,512]{3,2,1,0:T(8,128)} %w.5) | copy-start | bytes 786436
  11.6 12.3 %all-to-all-start = ((f32[4,4,4,8,128]{4,3,2,1,0:T(8,128)}), f32[4,4,4,8,128]{4,3,2,1,0:T(8,128)S(1)}, u32[]{:S(2)}, u32[]{:S(2)}) async-start(f32[4,4,4,8,128]{4,3,2,1,0:T(8,128)} %get-tuple-element.14), calls=%async_computation | async-start | bytes 524288 | tf_op jit(solution)/shard_map/all_to_all | solution.py:251
  61.4 17.3 %all-to-all-start.3 = ((f32[4,4,4,8,128]{4,3,2,1,0:T(8,128)}), f32[4,4,4,8,128]{4,3,2,1,0:T(8,128)S(1)}, u32[]{:S(2)}, u32[]{:S(2)}) async-start(f32[4,4,4,8,128]{4,3,2,1,0:T(8,128)} %get-tuple-element.23), calls=%async_computation.3 | async-start | bytes 524288 | tf_op jit(solution)/shard_map/all_to_all | solution.py:251
  66.3 7.1 %collective-permute-start.2 = (f32[4,4,4,512]{3,2,1,0:T(4,128)S(1)}, f32[4,4,4,512]{3,2,1,0:T(4,128)S(1)}, u32[]{:S(2)}, u32[]{:S(2)}) collective-permute-start(f32[4,4,4,512]{3,2,1,0:T(4,128)S(1)} %get-tuple-element.21), channel_id=1, source_target_pairs={{0,1},{1,0},{2,3},{3,2},{4,5},{5,4},{6,7},{7,6},{8,9},{9,8},{10,11... | collective-permute-start | bytes 393224 | tf_op jit(solution)/shard_map/ppermute | solution.py:327
  70.4 8.4 %collective-permute-start.3 = (f32[4,4,4,512]{3,2,1,0:T(4,128)S(1)}, f32[4,4,4,512]{3,2,1,0:T(4,128)S(1)}, u32[]{:S(2)}, u32[]{:S(2)}) collective-permute-start(f32[4,4,4,512]{3,2,1,0:T(4,128)S(1)} %get-tuple-element.22), channel_id=1, source_target_pairs={{1,2},{2,1},{3,4},{4,3},{5,6},{6,5},{7,8},{8,7},{9,10},{10,9},{11,... | collective-permute-start | bytes 393224 | tf_op jit(solution)/shard_map/ppermute | solution.py:326

commit v7 on v6

--- a/solution.py
+++ b/solution.py
@@ -96,13 +96,13 @@
         for j in range(1, members):
             colour = [colour[c] + transmit * agg[order[j], 1 + c, t] for c in range(3)]
             transmit = transmit * agg[order[j], 0, t]
-        for n in range(out.shape[0]):
-            out[n, 0, t] = transmit
-            for c in range(3):
-                out[n, 1 + c, t] = colour[c]
-
-
-def scan_kernel(place, agg, groups, w, out, shown):
+        out[0, t] = transmit
+        for c in range(3):
+            out[1 + c, t] = colour[c]
+
+
+def scan_kernel(place, agg, *refs):
+    parts, (w, out, shown) = refs[:-3], refs[-3:]
     members, _, tiles = agg.shape[:3]
     mine, owner, order = seat(place, members)
     bands = w.shape[2] // 8
@@ -114,17 +114,24 @@
         transmit = jnp.ones((8, LANES), jnp.float32)
         colour = [jnp.zeros((8, LANES), jnp.float32) for _ in range(3)]
         front = transmit
-        count = groups.shape[0]
+        count = len(parts)
+        own = [[part[c, t] for c in range(4)] for part in parts]
+        groups = []
+        for g in range(count):
+            found = own[g]
+            for h in range(1, count):
+                found = [jnp.where(mine == h, own[g ^ h][c], found[c]) for c in range(4)]
+            groups.append(found)
         for g in range(count):
             front = jnp.where(mine == g, transmit, front)
-            colour = [colour[c] + transmit * groups[g, 1 + c, t] for c in range(3)]
-            transmit = transmit * groups[g, 0, t]
+            colour = [colour[c] + transmit * groups[g][1 + c] for c in range(3)]
+            transmit = transmit * groups[g][0]
         picture = colour + [1.0 - transmit]
         behind = -weight[3]
         enter = behind
         for g in range(count - 1, 0, -1):
-            glow = sum(weight[c] * groups[g, 1 + c, t] for c in range(3))
-            behind = glow + groups[g, 0, t] * behind
+            glow = sum(weight[c] * groups[g][1 + c] for c in range(3))
+            behind = glow + groups[g][0] * behind
             enter = jnp.where(mine == g - 1, behind, enter)
         fronts = []
         for j in range(members):
@@ -238,7 +245,6 @@
     size = views * bands
     near = [[size * g + i for i in range(size)] for g in range(count // size)]
     near = [row[size // 2 :] + row[: size // 2] if g >= 2 else row for g, row in enumerate(near)]
-    far = [[row[i] for row in near] for i in range(size)]
     pairs = [(i, i ^ 1) for i in range(strips)]
     links = [(i, ((i + 1) ^ 1) - 1) for i in range(1, strips - 1)]
     f32 = lambda *shape: jax.ShapeDtypeStruct(shape, jnp.float32)
@@ -291,21 +297,25 @@
     agg = on_chip(agg)
     grouped = pl.pallas_call(
         group_kernel,
-        out_shape=kept(count // size, 4, tiles, 8, LANES),
+        out_shape=kept(4, tiles, 8, LANES),
         in_specs=[SMEM, VMEM],
         out_specs=VMEM,
         compiler_params=LIMIT,
         name="group",
     )(place, agg)
-    groups = on_chip(swap(grouped, far))
+    parts = {0: grouped}
+    for j in (2, 3, 1):
+        hops = [(a, b) for g, row in enumerate(near) for a, b in zip(row, near[g ^ j])]
+        parts[j] = lax.ppermute(grouped, "depth", hops)
+    parts = [on_chip(parts[j]) for j in range(count // size)]
     sent, shown = pl.pallas_call(
         scan_kernel,
         out_shape=(kept(size, 2, tiles, 8, LANES), kept(size, 4, tiles, 8, LANES)),
-        in_specs=[SMEM, VMEM, VMEM, VMEM],
+        in_specs=[SMEM] + [VMEM] * (2 + count // size),
         out_specs=(VMEM, VMEM),
         compiler_params=LIMIT,
         name="scan",
-    )(place, agg, groups, w)
+    )(place, agg, *parts, w)
     got = on_chip(swap(sent, near))
     shown = swap(shown, near)
 

time: 80.2 us -> 81.5 us (1.016)
  the two profiles are of different devices: /device:TPU:61 before, /device:TPU:57 now
where the time goes in v7:
time: 81.5 us; the launch traced here: 81 us
  starting transfers between devices  39.1 us (48%)
  waiting for transfers between devices  24.8 us (30%)
  blocking collectives  9.52 us (12%)
  Pallas kernels  5.61 us (7%)
  other arithmetic  1.14 us (1%)
    ppermute x3, starting transfers between devices, on_device(): parts[j] = lax.ppermute(grouped, 'depth', hops)  18.5 us
    ppermute x3, waiting for transfers between devices, on_device(): parts[j] = lax.ppermute(grouped, 'depth', hops)  10.1 us
    all_to_all x1, blocking collectives, swap(): lax.all_to_all(x, 'depth', 0, 0, tiled=True, axis_index_groups=groups)  9.52 us
    all_to_all x2, starting transfers between devices, swap(): lax.all_to_all(x, 'depth', 0, 0, tiled=True, axis_index_groups=groups)  9.5 us
    all_to_all x2, waiting for transfers between devices, swap(): lax.all_to_all(x, 'depth', 0, 0, tiled=True, axis_index_groups=groups)  6.02 us
    ppermute x1, waiting for transfers between devices, on_device(): from_outer = lax.ppermute(to_outer, 'lat', links)  5.64 us
    ppermute x1, starting transfers between devices, on_device(): from_inner = lax.ppermute(to_inner, 'lat', pairs)  3.98 us
    ppermute x1, starting transfers between devices, on_device(): outer = lax.ppermute(jnp.where(odd, last, first), 'lat', links)  3.34 us
  transfers between devices with their start and end apart: 9, of which 5 were waited for; matrix products, arithmetic and copies ran while one was open for 0% of the time, Pallas kernels for 3%

profile of v7, /device:TPU:57, one launch (start us, length us, event | category | flops | bytes accessed | tf_op | source)
XLA Modules:
  0.0 81.0 jit_solution(1782542927591094235)
XLA Ops:
  0.6 0.0 copy-start.1
  0.6 1.1 %slice_select_fusion = (f32[4,4,4,512]{3,2,1,0:T(4,128)S(1)}, f32[4,4,4,512]{3,2,1,0:T(4,128)S(1)}) fusion(f32[4,4,16,512]{3,2,1,0:T(8,128)} %vol.1, pred[]{:T(512)} %bitcast.3), kind=kLoop, calls=%fused_computation | loop fusion | flops 65536 | bytes 524289 | tf_op jit(solution)/shard_map/jit(_where)/select_n | solution.py:262
  1.8 3.3 %collective-permute-start.1 = (f32[4,4,4,512]{3,2,1,0:T(4,128)S(1)}, f32[4,4,4,512]{3,2,1,0:T(4,128)S(1)}, u32[]{:S(2)}, u32[]{:S(2)}) collective-permute-start(f32[4,4,4,512]{3,2,1,0:T(4,128)S(1)} %get-tuple-element.26), channel_id=1, source_target_pairs={{1,2},{2,1},{3,4},{4,3},{5,6},{6,5},{7,8},{8,7},{9,10},{10,9},{11,... | collective-permute-start | bytes 393224 | tf_op jit(solution)/shard_map/ppermute | solution.py:262
  5.1 1.9 %collective-permute-start = (f32[4,4,4,512]{3,2,1,0:T(4,128)S(1)}, f32[4,4,4,512]{3,2,1,0:T(4,128)S(1)}, u32[]{:S(2)}, u32[]{:S(2)}) collective-permute-start(f32[4,4,4,512]{3,2,1,0:T(4,128)S(1)} %get-tuple-element.27), channel_id=1, source_target_pairs={{0,1},{1,0},{2,3},{3,2},{4,5},{5,4},{6,7},{7,6},{8,9},{9,8},{10,11... | collective-permute-start | bytes 393224 | tf_op jit(solution)/shard_map/ppermute | solution.py:263
  7.1 0.0 copy-done.1
  7.1 0.0 copy-start.2
  7.1 0.0 copy-start.3
  7.1 3.0 %collective-permute-done.1.refs_4_ = f32[4,4,4,512]{3,2,1,0:T(4,128)S(1)} collective-permute-done((f32[4,4,4,512]{3,2,1,0:T(4,128)S(1)}, f32[4,4,4,512]{3,2,1,0:T(4,128)S(1)}, u32[]{:S(2)}, u32[]{:S(2)}) %collective-permute-start.1) | collective-permute-done | bytes 131104 | tf_op jit(solution)/shard_map/ppermute | solution.py:262
  10.2 0.0 collective-permute-done.refs_3_
  10.2 0.0 copy-done.2
  10.2 0.0 copy-done.3
  10.2 1.4 %slab.1 = (f32[4,4,4,8,128]{4,3,2,1,0:T(8,128)}, f32[4,4,4,32,128]{4,3,2,1,0:T(8,128)S(1)}) custom-call(s32[4,8]{1,0:T(4,128)S(1)} %bitcast.4, s32[2]{0:T(128)S(1)} %copy-done.3, s32[1]{0:T(128)} %bitcast.refs_2_.strip, f32[4,4,4,512]{3,2,1,0:T(4,128)S(1)} %collective-permute-done.refs_3_, ...), custom_call_target="tpu_custom_call", output_to_operand_aliasing={{1}: (5, {})} | custom-call | tf_op jit(solution)/shard_map/slab/pallas_call | solution.py:272
  11.6 0.0 copy-start
  11.6 5.6 %all-to-all-start = ((f32[4,4,4,8,128]{4,3,2,1,0:T(8,128)}), f32[4,4,4,8,128]{4,3,2,1,0:T(8,128)S(1)}, u32[]{:S(2)}, u32[]{:S(2)}) async-start(f32[4,4,4,8,128]{4,3,2,1,0:T(8,128)} %get-tuple-element.14), calls=%async_computation | async-start | bytes 524288 | tf_op jit(solution)/shard_map/all_to_all | solution.py:257
  17.2 0.0 copy-done
  17.2 0.7 local.1
  17.9 6.0 %all-to-all-done.agg = f32[4,4,4,8,128]{4,3,2,1,0:T(8,128)S(1)} async-done(((f32[4,4,4,8,128]{4,3,2,1,0:T(8,128)}), f32[4,4,4,8,128]{4,3,2,1,0:T(8,128)S(1)}, u32[]{:S(2)}, u32[]{:S(2)}) %all-to-all-start) | async-done | bytes 262176 | tf_op jit(solution)/shard_map/all_to_all | solution.py:257
  24.0 9.6 %collective-permute-start.4 = (f32[4,4,8,128]{3,2,1,0:T(8,128)S(1)}, f32[4,4,8,128]{3,2,1,0:T(8,128)S(1)}, u32[]{:S(2)}, u32[]{:S(2)}) collective-permute-start(f32[4,4,8,128]{3,2,1,0:T(8,128)S(1)} %group.1.refs_0_), channel_id=1, source_target_pairs={{0,448},{32,480},{64,384},{96,416},{128,320},{160,352},{192,256},{... | collective-permute-start | bytes 196616 | tf_op jit(solution)/shard_map/ppermute | solution.py:309
  33.6 6.3 %collective-permute-start.3 = (f32[4,4,8,128]{3,2,1,0:T(8,128)S(1)}, f32[4,4,8,128]{3,2,1,0:T(8,128)S(1)}, u32[]{:S(2)}, u32[]{:S(2)}) collective-permute-start(f32[4,4,8,128]{3,2,1,0:T(8,128)S(1)} %group.1.refs_0_), channel_id=1, source_target_pairs={{0,320},{32,352},{64,256},{96,288},{128,448},{160,480},{192,384},{... | collective-permute-start | bytes 196616 | tf_op jit(solution)/shard_map/ppermute | solution.py:309
  39.8 2.7 %collective-permute-start.2 = (f32[4,4,8,128]{3,2,1,0:T(8,128)S(1)}, f32[4,4,8,128]{3,2,1,0:T(8,128)S(1)}, u32[]{:S(2)}, u32[]{:S(2)}) collective-permute-start(f32[4,4,8,128]{3,2,1,0:T(8,128)S(1)} %group.1.refs_0_), channel_id=1, source_target_pairs={{0,128},{32,160},{64,192},{96,224},{128,0},{160,32},{192,64},{224,... | collective-permute-start | bytes 196616 | tf_op jit(solution)/shard_map/ppermute | solution.py:309
  42.5 0.0 collective-permute-done.4.refs_3_
  42.5 5.8 %collective-permute-done.3.refs_2_ = f32[4,4,8,128]{3,2,1,0:T(8,128)S(1)} collective-permute-done((f32[4,4,8,128]{3,2,1,0:T(8,128)S(1)}, f32[4,4,8,128]{3,2,1,0:T(8,128)S(1)}, u32[]{:S(2)}, u32[]{:S(2)}) %collective-permute-start.3) | collective-permute-done | bytes 65568 | tf_op jit(solution)/shard_map/ppermute | solution.py:309
  48.3 4.2 %collective-permute-done.2.refs_1_ = f32[4,4,8,128]{3,2,1,0:T(8,128)S(1)} collective-permute-done((f32[4,4,8,128]{3,2,1,0:T(8,128)S(1)}, f32[4,4,8,128]{3,2,1,0:T(8,128)S(1)}, u32[]{:S(2)}, u32[]{:S(2)}) %collective-permute-start.2) | collective-permute-done | bytes 65568 | tf_op jit(solution)/shard_map/ppermute | solution.py:309
  52.6 0.8 scan.1
  53.4 9.5 %all_to_all.15.got = f32[4,2,4,8,128]{4,3,2,1,0:T(8,128)S(1)} all-to-all(f32[4,2,4,8,128]{4,3,2,1,0:T(8,128)S(1)} %get-tuple-element.18), channel_id=1, replica_groups={{0,32,64,96},{128,160,192,224},{320,352,256,288},{448,480,384,416},{1,3..., dimensions={0} | all-to-all | bytes 262144 | tf_op jit(solution)/shard_map/all_to_all | solution.py:257
  62.9 3.9 %all-to-all-start.2 = ((f32[4,4,4,8,128]{4,3,2,1,0:T(8,128)}), f32[4,4,4,8,128]{4,3,2,1,0:T(8,128)S(1)}, u32[]{:S(2)}, u32[]{:S(2)}) async-start(f32[4,4,4,8,128]{4,3,2,1,0:T(8,128)} %get-tuple-element.23), calls=%async_computation.2 | async-start | bytes 524288 | tf_op jit(solution)/shard_map/all_to_all | solution.py:257
  66.8 0.8 edge.1
  67.6 4.0 %collective-permute-start.5 = (f32[4,4,4,512]{3,2,1,0:T(4,128)S(1)}, f32[4,4,4,512]{3,2,1,0:T(4,128)S(1)}, u32[]{:S(2)}, u32[]{:S(2)}) collective-permute-start(f32[4,4,4,512]{3,2,1,0:T(4,128)S(1)} %get-tuple-element.21), channel_id=1, source_target_pairs={{0,1},{1,0},{2,3},{3,2},{4,5},{5,4},{6,7},{7,6},{8,9},{9,8},{10,11... | collective-permute-start | bytes 393224 | tf_op jit(solution)/shard_map/ppermute | solution.py:337
  71.6 1.9 %collective-permute-start.6 = (f32[4,4,4,512]{3,2,1,0:T(4,128)S(1)}, f32[4,4,4,512]{3,2,1,0:T(4,128)S(1)}, u32[]{:S(2)}, u32[]{:S(2)}) collective-permute-start(f32[4,4,4,512]{3,2,1,0:T(4,128)S(1)} %get-tuple-element.22), channel_id=1, source_target_pairs={{1,2},{2,1},{3,4},{4,3},{5,6},{6,5},{7,8},{8,7},{9,10},{10,9},{11,... | collective-permute-start | bytes 393224 | tf_op jit(solution)/shard_map/ppermute | solution.py:336
  73.5 0.8 %main.1 = f32[4,4,16,512]{3,2,1,0:T(8,128)S(1)} custom-call(s32[4,8]{1,0:T(4,128)S(1)} %bitcast.7, s32[2]{0:T(128)S(1)} %copy-done.3, f32[4,2,4,8,128]{4,3,2,1,0:T(8,128)S(1)} %all_to_all.15.got, f32[2,4,4,16,128]{4,3,2,1,0:T(8,128)S(1)} %get-tuple-element.19.absorb_part, f32[2,4,4,16,128]{4,3,2,1,0:T(8,128)S(1)} %get-tuple-element.20.emit_part, ...), custom_call_target="tpu_custom_call" | custom-call | tf_op jit(solution)/shard_map/main/pallas_call | solution.py:338
  74.3 0.0 collective-permute-done.5.inner
  74.4 5.6 %collective-permute-done.6.outer = f32[4,4,4,512]{3,2,1,0:T(4,128)S(1)} collective-permute-done((f32[4,4,4,512]{3,2,1,0:T(4,128)S(1)}, f32[4,4,4,512]{3,2,1,0:T(4,128)S(1)}, u32[]{:S(2)}, u32[]{:S(2)}) %collective-permute-start.6) | collective-permute-done | bytes 131104 | tf_op jit(solution)/shard_map/ppermute | solution.py:336
  80.0 0.0 all-to-all-done.2.shown
  80.0 1.0 %join.1 = (f32[4,4,16,512]{3,2,1,0:T(8,128)}, f32[2,4,16,512]{3,2,1,0:T(8,128)}) custom-call(s32[1]{0:T(128)} %bitcast.refs_2_.strip, f32[4,4,16,512]{3,2,1,0:T(8,128)S(1)} %main.1, f32[4,4,4,512]{3,2,1,0:T(4,128)S(1)} %collective-permute-done.5.inner, f32[4,4,4,512]{3,2,1,0:T(4,128)S(1)} %collective-permute-done.6.outer, ...), custom_call_target="tpu_custom_call" | custom-call | tf_op jit(solution)/shard_map/join/pallas_call | solution.py:349
  (2 shorter events, 0.1 us)
Async XLA Ops:
  0.6 6.4 %copy-start.1 = (f32[4,4,16,512]{3,2,1,0:T(8,128)S(1)}, f32[4,4,16,512]{3,2,1,0:T(8,128)}, u32[]{:S(2)}) copy-start(f32[4,4,16,512]{3,2,1,0:T(8,128)} %vol.1) | copy-start | bytes 1572868
  1.8 8.4 %collective-permute-start.1 = (f32[4,4,4,512]{3,2,1,0:T(4,128)S(1)}, f32[4,4,4,512]{3,2,1,0:T(4,128)S(1)}, u32[]{:S(2)}, u32[]{:S(2)}) collective-permute-start(f32[4,4,4,512]{3,2,1,0:T(4,128)S(1)} %get-tuple-element.26), channel_id=1, source_target_pairs={{1,2},{2,1},{3,4},{4,3},{5,6},{6,5},{7,8},{8,7},{9,10},{10,9},{11,... | collective-permute-start | bytes 393224 | tf_op jit(solution)/shard_map/ppermute | solution.py:262
  5.1 5.1 %collective-permute-start = (f32[4,4,4,512]{3,2,1,0:T(4,128)S(1)}, f32[4,4,4,512]{3,2,1,0:T(4,128)S(1)}, u32[]{:S(2)}, u32[]{:S(2)}) collective-permute-start(f32[4,4,4,512]{3,2,1,0:T(4,128)S(1)} %get-tuple-element.27), channel_id=1, source_target_pairs={{0,1},{1,0},{2,3},{3,2},{4,5},{5,4},{6,7},{7,6},{8,9},{9,8},{10,11... | collective-permute-start | bytes 393224 | tf_op jit(solution)/shard_map/ppermute | solution.py:263
  7.1 3.1 %copy-start.2 = (s32[8,4]{0,1:T(4,128)S(1)}, s32[8,4]{0,1:T(4,128)}, u32[]{:S(2)}) copy-start(s32[8,4]{0,1:T(4,128)} %param.5) | copy-start | bytes 388
  7.1 3.1 %copy-start.3 = (s32[2]{0:T(128)S(1)}, s32[2]{0:T(128)}, u32[]{:S(2)}) copy-start(s32[2]{0:T(128)} %vids.3) | copy-start | bytes 28
  11.6 5.6 %copy-start = (f32[2,4,16,512]{3,2,1,0:T(8,128)S(1)}, f32[2,4,16,512]{3,2,1,0:T(8,128)}, u32[]{:S(2)}) copy-start(f32[2,4,16,512]{3,2,1,0:T(8,128)} %w.3) | copy-start | bytes 786436
  11.6 12.3 %all-to-all-start = ((f32[4,4,4,8,128]{4,3,2,1,0:T(8,128)}), f32[4,4,4,8,128]{4,3,2,1,0:T(8,128)S(1)}, u32[]{:S(2)}, u32[]{:S(2)}) async-start(f32[4,4,4,8,128]{4,3,2,1,0:T(8,128)} %get-tuple-element.14), calls=%async_computation | async-start | bytes 524288 | tf_op jit(solution)/shard_map/all_to_all | solution.py:257
  24.0 18.5 %collective-permute-start.4 = (f32[4,4,8,128]{3,2,1,0:T(8,128)S(1)}, f32[4,4,8,128]{3,2,1,0:T(8,128)S(1)}, u32[]{:S(2)}, u32[]{:S(2)}) collective-permute-start(f32[4,4,8,128]{3,2,1,0:T(8,128)S(1)} %group.1.refs_0_), channel_id=1, source_target_pairs={{0,448},{32,480},{64,384},{96,416},{128,320},{160,352},{192,256},{... | collective-permute-start | bytes 196616 | tf_op jit(solution)/shard_map/ppermute | solution.py:309
  33.6 14.8 %collective-permute-start.3 = (f32[4,4,8,128]{3,2,1,0:T(8,128)S(1)}, f32[4,4,8,128]{3,2,1,0:T(8,128)S(1)}, u32[]{:S(2)}, u32[]{:S(2)}) collective-permute-start(f32[4,4,8,128]{3,2,1,0:T(8,128)S(1)} %group.1.refs_0_), channel_id=1, source_target_pairs={{0,320},{32,352},{64,256},{96,288},{128,448},{160,480},{192,384},{... | collective-permute-start | bytes 196616 | tf_op jit(solution)/shard_map/ppermute | solution.py:309
  39.8 12.7 %collective-permute-start.2 = (f32[4,4,8,128]{3,2,1,0:T(8,128)S(1)}, f32[4,4,8,128]{3,2,1,0:T(8,128)S(1)}, u32[]{:S(2)}, u32[]{:S(2)}) collective-permute-start(f32[4,4,8,128]{3,2,1,0:T(8,128)S(1)} %group.1.refs_0_), channel_id=1, source_target_pairs={{0,128},{32,160},{64,192},{96,224},{128,0},{160,32},{192,64},{224,... | collective-permute-start | bytes 196616 | tf_op jit(solution)/shard_map/ppermute | solution.py:309
  62.9 17.1 %all-to-all-start.2 = ((f32[4,4,4,8,128]{4,3,2,1,0:T(8,128)}), f32[4,4,4,8,128]{4,3,2,1,0:T(8,128)S(1)}, u32[]{:S(2)}, u32[]{:S(2)}) async-start(f32[4,4,4,8,128]{4,3,2,1,0:T(8,128)} %get-tuple-element.23), calls=%async_computation.2 | async-start | bytes 524288 | tf_op jit(solution)/shard_map/all_to_all | solution.py:257
  67.6 6.7 %collective-permute-start.5 = (f32[4,4,4,512]{3,2,1,0:T(4,128)S(1)}, f32[4,4,4,512]{3,2,1,0:T(4,128)S(1)}, u32[]{:S(2)}, u32[]{:S(2)}) collective-permute-start(f32[4,4,4,512]{3,2,1,0:T(4,128)S(1)} %get-tuple-element.21), channel_id=1, source_target_pairs={{0,1},{1,0},{2,3},{3,2},{4,5},{5,4},{6,7},{7,6},{8,9},{9,8},{10,11... | collective-permute-start | bytes 393224 | tf_op jit(solution)/shard_map/ppermute | solution.py:337
  71.6 8.4 %collective-permute-start.6 = (f32[4,4,4,512]{3,2,1,0:T(4,128)S(1)}, f32[4,4,4,512]{3,2,1,0:T(4,128)S(1)}, u32[]{:S(2)}, u32[]{:S(2)}) collective-permute-start(f32[4,4,4,512]{3,2,1,0:T(4,128)S(1)} %get-tuple-element.22), channel_id=1, source_target_pairs={{1,2},{2,1},{3,4},{4,3},{5,6},{6,5},{7,8},{8,7},{9,10},{10,9},{11,... | collective-permute-start | bytes 393224 | tf_op jit(solution)/shard_map/ppermute | solution.py:336
